TPU v7x, 256 devices: a whole 4x4x8 slice. The times are simulated.
256 devices in a mesh: lat: 32 (over y, z_lo, x), lev: 8 (over z_hi, core).
Axes of the slice: x: 4, y: 4, z: 8 (z_hi: 4, z_lo: 2; z = z_hi * 2 + z_lo), core: 2. Of those that a mesh axis runs over, the one named last changes fastest.
Arguments:
- prognostic: float32 [4, 24, 256, 768], P(None, 'lev', 'lat'), may hold values from -6 to 6
- cotangent: bfloat16 [4, 24, 256, 768], P(None, 'lev', 'lat'), may hold values from -6 to 6
- damping: float32 [4, 24], P(None, 'lev'), may hold values from 1 to 30
- in_scale: float32 [4, 24], replicated, may hold values from 0.5 to 4
- w_in: bfloat16 [512, 96], replicated, may hold values from -0.625 to 0.625
- b_in: float32 [512], replicated, may hold values from -3 to 3
- w_mid: bfloat16 [512, 512], replicated, may hold values from -0.25 to 0.25
- b_mid: float32 [512], replicated, may hold values from -3 to 3
- w_out: bfloat16 [96, 512], replicated, may hold values from -0.25 to 0.25
- wave_order: int32 [256], replicated, may hold values from 0 to 255, as said below
- lat_order: int32 [256], replicated, may hold values from 0 to 255, each once
Outputs:
- new_state: float32 [4, 24, 256, 768], P(None, 'lev', 'lat')
- spectral: float32 [256, 2, 4, 24, 256], P('lat', None, None, 'lev')
- grad_w_in: float32 [512, 96], replicated
- grad_b_in: float32 [512], replicated
- grad_w_mid: float32 [512, 512], replicated
- grad_b_mid: float32 [512], replicated
- grad_w_out: float32 [96, 512], replicated
Inputs may be any that keep to these rules, and one draw needn't show every extreme that they name: `wave_order`: A permutation of the wavenumbers. Block d, entries d * 8 to (d + 1) * 8 - 1, lists the wavenumbers owned by index d of lat: one from each run of 32 consecutive wavenumbers, taken from alternate ends of the runs so that the triangular work of the blocks is nearly equal. `lat_order`: A permutation of the latitudes.
All inputs are finite; a program needn't handle non-finite values.
Results may differ from a plain program's by a relative error of at most 0.006.
Values may be sent and summed in bfloat16 or wider, within the bound.
A program may use at most 64 MiB of HBM per device.

v0:
```python
import math

import jax
import jax.numpy as jnp
from jax import lax
from jax.sharding import PartitionSpec as P

TRUNC = 256


block_rows = 32
rescale_bits = 40.0


def legendre_setup(own_waves, colatitude):
    float_type = colatitude.dtype
    all_orders = jnp.arange(TRUNC, dtype=jnp.int32)
    factor_index = jnp.arange(1, TRUNC, dtype=jnp.int32).astype(float_type)
    ratios = 0.5 * jnp.log((2.0 * factor_index + 1.0) / (2.0 * factor_index))
    totals = jnp.concatenate([jnp.zeros((1,), float_type), jnp.cumsum(ratios)])
    matches = own_waves[:, None] == all_orders[None, :]
    diagonal_log = jnp.sum(jnp.where(matches, totals[None, :], 0.0), axis=1) - 0.5 * math.log(2.0)
    orders = own_waves.astype(float_type)
    log_shift = diagonal_log[:, None] + orders[:, None] * jnp.log(jnp.sin(colatitude))[None, :]
    empty_rows = jnp.zeros_like(log_shift)
    return (empty_rows, empty_rows, log_shift)


def legendre_rows(recurrence, first_degree, orders, cosine):
    latest, before, log_shift = recurrence
    rescale_limit = 2.0**rescale_bits
    squared_order = orders * orders
    table_rows = []
    for offset in range(block_rows):
        degree = (first_degree + offset).astype(cosine.dtype)
        upper_coef = jnp.sqrt(
            jnp.maximum(4.0 * degree * degree - 1.0, 0.0)
            / jnp.maximum(degree * degree - squared_order, 1.0)
        )
        lower_num = jnp.maximum((degree - 1.0) * (degree - 1.0) - squared_order, 0.0)
        lower_coef = jnp.sqrt(
            lower_num / jnp.maximum(4.0 * (degree - 1.0) * (degree - 1.0) - 1.0, 1.0)
        )
        recurred = upper_coef[:, None] * (cosine[None, :] * latest - lower_coef[:, None] * before)
        diagonal_start = jnp.where(degree == orders, 1.0, 0.0)[:, None] * jnp.ones_like(latest)
        newest = jnp.where((degree > orders)[:, None], recurred, diagonal_start)
        too_large = jnp.abs(newest) > rescale_limit
        factor = jnp.where(too_large, 1.0 / rescale_limit, 1.0)
        newest = newest * factor
        latest = latest * factor
        log_shift = log_shift + jnp.where(too_large, rescale_bits * math.log(2.0), 0.0)
        table_rows.append(newest * jnp.exp(log_shift))
        before = latest
        latest = newest
    return ((latest, before, log_shift), jnp.stack(table_rows, axis=1))


def spectral_pass(own_waves, colatitude, fourier, damping):
    float_type = fourier.dtype
    lat_total = colatitude.shape[0]
    weight = math.pi / lat_total * jnp.sin(colatitude)
    cosine = jnp.cos(colatitude)
    orders = own_waves.astype(float_type)
    weighted = fourier * weight
    degree_norm = 1.0 / (TRUNC * (TRUNC - 1.0))

    def visit_block(carried, first_degree):
        recurrence, grid_sum = carried
        recurrence, legendre_table = legendre_rows(recurrence, first_degree, orders, cosine)
        coeffs = jnp.einsum(
            "jbn,jkfen->jkfeb", legendre_table, weighted, precision=lax.Precision.HIGHEST
        )
        degree = (first_degree + jnp.arange(block_rows, dtype=jnp.int32)).astype(float_type)
        degree_ratio = degree * (degree + 1.0) * degree_norm
        coeffs = coeffs / (1.0 + damping[:, :, None] * (degree_ratio * degree_ratio)[None, None, :])
        grid_sum = grid_sum + jnp.einsum(
            "jbn,jkfeb->jkfen", legendre_table, coeffs, precision=lax.Precision.HIGHEST
        )
        return ((recurrence, grid_sum), coeffs)

    starts = jnp.arange(0, TRUNC, block_rows, dtype=jnp.int32)
    initial = (legendre_setup(own_waves, colatitude), jnp.zeros_like(fourier))
    (recurrence, synthesized), blocks = lax.scan(visit_block, initial, starts)
    waves, two, fields, levels = fourier.shape[:4]
    coeffs = jnp.moveaxis(blocks, 0, 4).reshape(waves, two, fields, levels, TRUNC)
    return (coeffs, synthesized)


def fourier_angles(wave_order, lon_count):
    points = jnp.arange(lon_count, dtype=jnp.int32)
    phase_index = wave_order[:, None] * points[None, :] % lon_count
    return phase_index.astype(jnp.float32) * (2.0 * math.pi / lon_count)


def fourier_forward(wave_order, lon_count):
    angles = fourier_angles(wave_order, lon_count)
    return jnp.stack([jnp.cos(angles), -jnp.sin(angles)], axis=1) / lon_count


def fourier_inverse(wave_order, lon_count):
    angles = fourier_angles(wave_order, lon_count)
    weights = jnp.where(wave_order == 0, 1.0, 2.0)[:, None, None]
    return weights * jnp.stack([jnp.cos(angles), -jnp.sin(angles)], axis=1)


def silu_slope(value):
    sigmoid_value = jax.nn.sigmoid(value)
    return sigmoid_value * (1.0 + value * (1.0 - sigmoid_value))


def column_physics(inputs, upstream, w_in, b_in, w_mid, b_mid, w_out):
    pre_in = jnp.dot(w_in, inputs, preferred_element_type=jnp.float32) + b_in[:, None]
    hidden_in = jax.nn.silu(pre_in).astype(jnp.bfloat16)
    pre_mid = jnp.dot(w_mid, hidden_in, preferred_element_type=jnp.float32) + b_mid[:, None]
    hidden_mid = jax.nn.silu(pre_mid).astype(jnp.bfloat16)
    tendency = jnp.dot(w_out, hidden_mid, preferred_element_type=jnp.float32).astype(jnp.bfloat16)
    grad_out = jnp.dot(upstream, hidden_mid.T, preferred_element_type=jnp.float32)
    back_mid = jnp.dot(w_out.T, upstream, preferred_element_type=jnp.float32)
    delta_mid = (back_mid * silu_slope(pre_mid)).astype(jnp.bfloat16)
    grad_mid = jnp.dot(delta_mid, hidden_in.T, preferred_element_type=jnp.float32)
    grad_bmid = jnp.sum(delta_mid.astype(jnp.float32), axis=1)
    back_in = jnp.dot(w_mid.T, delta_mid, preferred_element_type=jnp.float32)
    delta_in = (back_in * silu_slope(pre_in)).astype(jnp.bfloat16)
    grad_in = jnp.dot(delta_in, inputs.T, preferred_element_type=jnp.float32)
    grad_bin = jnp.sum(delta_in.astype(jnp.float32), axis=1)
    return (tendency, (grad_in, grad_bin, grad_mid, grad_bmid, grad_out))


def physics_rows(inputs, upstream, w_in, b_in, w_mid, b_mid, w_out):
    fields, lev_total, lat_rows, lon_count = inputs.shape
    features = fields * lev_total
    hidden_units = w_in.shape[0]
    rows_in = jnp.moveaxis(inputs.reshape(features, lat_rows, lon_count), 1, 0)
    rows_up = jnp.moveaxis(upstream.reshape(features, lat_rows, lon_count), 1, 0)

    def visit_row(totals, row_pair):
        tendency, gradients = column_physics(
            row_pair[0], row_pair[1], w_in, b_in, w_mid, b_mid, w_out
        )
        return (jax.tree.map(jnp.add, totals, gradients), tendency)

    empty_sums = (
        jnp.zeros((hidden_units, features), jnp.float32),
        jnp.zeros((hidden_units,), jnp.float32),
        jnp.zeros((hidden_units, hidden_units), jnp.float32),
        jnp.zeros((hidden_units,), jnp.float32),
        jnp.zeros((features, hidden_units), jnp.float32),
    )
    totals, tend_rows = lax.scan(visit_row, empty_sums, (rows_in, rows_up))
    tendency = jnp.moveaxis(tend_rows, 0, 1).reshape(fields, lev_total, lat_rows, lon_count)
    return (tendency, totals)


def on_device(
    prognostic, cotangent, damping, in_scale, w_in, b_in, w_mid, b_mid, w_out, wave_order, lat_order
):
    fields, lev_dev, lat_dev, lon_count = prognostic.shape
    lat_width = lax.axis_size("lat")
    wave_dev = wave_order.shape[0] // lat_width
    lat_total = lat_order.shape[0]
    my_index = lax.axis_index("lat")
    own_waves = lax.dynamic_slice_in_dim(wave_order, my_index * wave_dev, wave_dev)
    to_fourier = fourier_forward(wave_order, lon_count)
    fourier = jnp.einsum("jkn,fean->jkfea", to_fourier, prognostic, precision=lax.Precision.HIGHEST)
    fourier = lax.all_to_all(fourier, "lat", split_axis=0, concat_axis=4, tiled=True)
    colatitude = math.pi * (lat_order.astype(jnp.float32) + 0.5) / lat_total
    spectral, synthesized = spectral_pass(own_waves, colatitude, fourier, damping)
    upstream = lax.all_to_all(cotangent, "lev", split_axis=2, concat_axis=1, tiled=True)
    from_fourier = fourier_inverse(wave_order, lon_count)
    row_modes = lax.all_to_all(synthesized, "lat", split_axis=4, concat_axis=0, tiled=True)
    filtered = jnp.einsum(
        "jkfea,jkn->fean", row_modes, from_fourier, precision=lax.Precision.HIGHEST
    )
    lev_index = lax.axis_index("lev")
    local_scale = lax.dynamic_slice_in_dim(in_scale, lev_index * lev_dev, lev_dev, 1)
    local_inputs = (filtered * local_scale[:, :, None, None]).astype(jnp.bfloat16)
    inputs = lax.all_to_all(local_inputs, "lev", split_axis=2, concat_axis=1, tiled=True)
    tend_cols, totals = physics_rows(inputs, upstream, w_in, b_in, w_mid, b_mid, w_out)
    tendency = lax.all_to_all(tend_cols, "lev", split_axis=1, concat_axis=2, tiled=True)
    new_state = filtered + tendency.astype(jnp.float32)
    grad_scale = 1.0 / math.sqrt(lat_total * lon_count)
    summed = lax.psum(
        (
            totals[0] * grad_scale,
            totals[1] * grad_scale,
            totals[2] * grad_scale,
            totals[3] * grad_scale,
            totals[4] * grad_scale,
        ),
        ("lat", "lev"),
    )
    return (new_state, spectral, summed[0], summed[1], summed[2], summed[3], summed[4])


def solution(mesh):
    return jax.shard_map(
        on_device,
        mesh=mesh,
        in_specs=(
            P(None, "lev", "lat", None),
            P(None, "lev", "lat", None),
            P(None, "lev"),
            P(),
            P(),
            P(),
            P(),
            P(),
            P(),
            P(),
            P(),
        ),
        out_specs=(
            P(None, "lev", "lat", None),
            P("lat", None, None, "lev", None),
            P(),
            P(),
            P(),
            P(),
            P(),
        ),
        check_vma=False,
    )
```

profile of v0, /device:TPU:1, one launch (start us, length us, event | category | flops | bytes accessed | tf_op | source)
XLA Modules:
  0.0 603.7 jit_solution(1936918069799120080)
XLA Ops:
  7.2 4.0 fusion.160
  11.2 1.7 fusion.134
  12.9 2.8 copy.225
  15.7 5.7 reshape.1597
  21.4 9.4 %all-to-all-start = ((f32[32,1,1536]{2,1,0:T(1,128)}), f32[32,1,1536]{2,1,0:T(1,128)S(1)}, u32[]{:S(2)}, u32[]{:S(2)}) async-start(f32[32,1,1536]{2,1,0:T(1,128)} %reshape.1597), calls=%async_computation | async-start | bytes 393216 | tf_op jit(solution)/shard_map/all_to_all | solution.py:165
  32.1 6.6 %all-to-all-done = f32[32,1,1536]{2,1,0:T(1,128)S(1)} async-done(((f32[32,1,1536]{2,1,0:T(1,128)}), f32[32,1,1536]{2,1,0:T(1,128)S(1)}, u32[]{:S(2)}, u32[]{:S(2)}) %all-to-all-start) | async-done | bytes 196640 | tf_op jit(solution)/shard_map/all_to_all | solution.py:165
  39.2 1.1 reduce.2
  40.3 5.4 reshape.1598
  45.7 5.4 copy.260
  51.1 3.3 all_to_all.58
  54.6 211.2 %while.6 = (s32[]{:T(128)}, f32[8,256]{1,0:T(8,128)S(1)}, f32[8,256]{1,0:T(8,128)S(1)}, f32[8,256]{1,0:T(8,128)S(1)}, f32[8,2,4,3,256]{4,2,3,1,0:T(4,128)S(1)}, ...) while((s32[]{:T(128)}, f32[8,256]{1,0:T(8,128)S(1)}, ...), condition=%wide.region_4.5_spmd.clone, body=%wide.region_3.4_spmd.clone.sunk | while | flops 39038560 | bytes 3434068 | solution.py:83
  76.7 0.7 exponential_multiply_fusion.2
  78.7 0.7 fusion.230
  79.4 1.1 bitcast_dynamic-update-slice_fusion.2
  103.1 0.7 exponential_multiply_fusion.2
  105.1 0.7 fusion.230
  105.8 1.1 bitcast_dynamic-update-slice_fusion.2
  129.5 0.7 exponential_multiply_fusion.2
  131.5 0.7 fusion.230
  132.2 1.1 bitcast_dynamic-update-slice_fusion.2
  155.9 0.7 exponential_multiply_fusion.2
  157.9 0.7 fusion.230
  158.6 1.1 bitcast_dynamic-update-slice_fusion.2
  182.3 0.7 exponential_multiply_fusion.2
  184.3 0.7 fusion.230
  185.0 1.1 bitcast_dynamic-update-slice_fusion.2
  208.7 0.7 exponential_multiply_fusion.2
  210.7 0.7 fusion.230
  211.4 1.1 bitcast_dynamic-update-slice_fusion.2
  235.1 0.7 exponential_multiply_fusion.2
  237.1 0.7 fusion.230
  237.8 1.1 bitcast_dynamic-update-slice_fusion.2
  261.5 0.7 exponential_multiply_fusion.2
  263.5 0.7 fusion.230
  264.2 1.1 bitcast_dynamic-update-slice_fusion.2
  265.8 2.8 copy.230
  268.6 5.9 reshape.1599
  274.5 3.9 all-to-all-start.1
  278.5 0.7 copy.240
  279.2 6.9 %all-to-all-done.1 = f32[32,1,1536]{2,1,0:T(1,128)S(1)} async-done(((f32[32,1,1536]{2,1,0:T(1,128)}), f32[32,1,1536]{2,1,0:T(1,128)S(1)}, u32[]{:S(2)}, u32[]{:S(2)}) %all-to-all-start.1) | async-done | bytes 196640 | tf_op jit(solution)/shard_map/all_to_all | solution.py:170
  286.1 10.7 %all-to-all-start.4 = ((bf16[4,3,8,768]{3,0,1,2:T(4,128)(2,1)}), bf16[4,3,8,768]{3,0,1,2:T(4,128)(2,1)S(1)}, u32[]{:S(2)}, u32[]{:S(2)}) async-start(bf16[4,3,8,768]{3,0,1,2:T(4,128)(2,1)} %copy.240), calls=%async_computation.4 | async-start | bytes 294912 | tf_op jit(solution)/shard_map/all_to_all | solution.py:168
  296.8 1.1 reduce.3
  297.9 5.4 reshape.1600
  303.3 5.4 copy.259
  308.7 3.3 all_to_all.62
  312.1 1.1 fusion.132
  313.3 0.7 copy.235
  314.0 7.2 %all-to-all-start.2 = ((bf16[4,3,8,768]{3,0,1,2:T(4,128)(2,1)}), bf16[4,3,8,768]{3,0,1,2:T(4,128)(2,1)S(1)}, u32[]{:S(2)}, u32[]{:S(2)}) async-start(bf16[4,3,8,768]{3,0,1,2:T(4,128)(2,1)} %copy.235), calls=%async_computation.2 | async-start | bytes 294912 | tf_op jit(solution)/shard_map/all_to_all | solution.py:177
  321.7 7.8 %all-to-all-done.2 = bf16[4,3,8,768]{3,0,1,2:T(4,128)(2,1)S(1)} async-done(((bf16[4,3,8,768]{3,0,1,2:T(4,128)(2,1)}), bf16[4,3,8,768]{3,0,1,2:T(4,128)(2,1)S(1)}, u32[]{:S(2)}, u32[]{:S(2)}) %all-to-all-start.2) | async-done | bytes 147488 | tf_op jit(solution)/shard_map/all_to_all | solution.py:177
  330.2 0.9 fusion.140
  331.1 0.8 convert_reduce_fusion
  331.9 0.9 convert_reduce_fusion.1
  332.8 1.7 convolution_multiply_fusion
  334.5 0.9 convolution_multiply_fusion.2
  335.4 0.9 fusion.153
  336.8 0.7 copy.237
  337.5 4.2 all-to-all-start.3
  342.2 1.0 reshape.1588
  343.2 75.9 %all-reduce.1 = (f32[512]{0:T(512)}, f32[512]{0:T(512)}) all-reduce(f32[512]{0:T(512)S(1)} %get-tuple-element.764, f32[512]{0:T(512)S(1)} %get-tuple-element.763), channel_id=1, replica_groups=mesh['lat'=32,'lev'=8] {'lat','lev'}, use_global_device_ids=true, to_apply=%region_7.8 | all-reduce | flops 1024 | bytes 8192 | tf_op jit(solution)/shard_map/psum | solution.py:182
  419.1 0.7 copy.243
  419.9 172.0 %all-reduce.5.cloned.1.call-done = (f32[512,96]{0,1:T(8,128)}, f32[512,512]{1,0:T(8,128)}, f32[96,512]{1,0:T(8,128)}) async-done(((f32[512,96]{0,1:T(8,128)}, f32[512,512]{1,0:T(8,128)}, f32[96,512]{1,0:T(8,128)}), (f32[512,96]{0,1:T(8,128)}, f32[512,512]{1,0:T(8,128)}, f32[96,512]{1,0:T(8,128)})) %all-reduce.5.cloned.1.call-update) | async-done | bytes 1441808 | tf_op jit(solution)/shard_map/psum | solution.py:182
  591.8 1.7 copy.345
  593.5 2.3 copy.346
  595.8 0.7 copy.347
  (531 shorter events, 23.4 us)
Async XLA Ops:
  7.2 323.0 %copy-start = (bf16[512,512]{1,0:T(8,128)(2,1)S(1)}, bf16[512,512]{1,0:T(8,128)(2,1)}, u32[]{:S(2)}) copy-start(bf16[512,512]{1,0:T(8,128)(2,1)} %param.19) | copy-start | bytes 1572868
  7.2 4.0 copy-start.2
  15.7 15.1 %copy-start.7 = (s32[256]{0:T(256)S(1)}, s32[256]{0:T(256)}, u32[]{:S(2)}) copy-start(s32[256]{0:T(256)} %param.22) | copy-start | bytes 3076
  15.7 15.8 %copy-start.11 = (s32[256]{0:T(256)S(1)}, s32[256]{0:T(256)}, u32[]{:S(2)}) copy-start(s32[256]{0:T(256)} %param.23) | copy-start | bytes 3076
  15.7 16.2 %copy-start.8 = (f32[4,3]{1,0:T(4,128)S(1)}, f32[4,3]{1,0:T(4,128)}, u32[]{:S(2)}) copy-start(f32[4,3]{1,0:T(4,128)} %param.15) | copy-start | bytes 148
  21.4 17.3 %all-to-all-start = ((f32[32,1,1536]{2,1,0:T(1,128)}), f32[32,1,1536]{2,1,0:T(1,128)S(1)}, u32[]{:S(2)}, u32[]{:S(2)}) async-start(f32[32,1,1536]{2,1,0:T(1,128)} %reshape.1597), calls=%async_computation | async-start | bytes 393216 | tf_op jit(solution)/shard_map/all_to_all | solution.py:165
  268.6 9.8 %copy-start.9 = (f32[4,24]{1,0:T(4,128)S(1)}, f32[4,24]{1,0:T(4,128)}, u32[]{:S(2)}) copy-start(f32[4,24]{1,0:T(4,128)} %param.16) | copy-start | bytes 1156
  268.6 9.9 %copy-start.4 = (bf16[4,3,8,768]{3,2,1,0:T(8,128)(2,1)S(1)}, bf16[4,3,8,768]{3,2,1,0:T(8,128)(2,1)}, u32[]{:S(2)}) copy-start(bf16[4,3,8,768]{3,2,1,0:T(8,128)(2,1)} %param.14) | copy-start | bytes 442372
  274.5 11.6 %all-to-all-start.1 = ((f32[32,1,1536]{2,1,0:T(1,128)}), f32[32,1,1536]{2,1,0:T(1,128)S(1)}, u32[]{:S(2)}, u32[]{:S(2)}) async-start(f32[32,1,1536]{2,1,0:T(1,128)} %reshape.1599), calls=%async_computation.1 | async-start | bytes 393216 | tf_op jit(solution)/shard_map/all_to_all | solution.py:170
  286.1 27.9 %all-to-all-start.4 = ((bf16[4,3,8,768]{3,0,1,2:T(4,128)(2,1)}), bf16[4,3,8,768]{3,0,1,2:T(4,128)(2,1)S(1)}, u32[]{:S(2)}, u32[]{:S(2)}) async-start(bf16[4,3,8,768]{3,0,1,2:T(4,128)(2,1)} %copy.240), calls=%async_computation.4 | async-start | bytes 294912 | tf_op jit(solution)/shard_map/all_to_all | solution.py:168
  313.2 16.6 %copy-start.5 = (bf16[512,96]{0,1:T(8,128)(2,1)S(1)}, bf16[512,96]{0,1:T(8,128)(2,1)}, u32[]{:S(2)}) copy-start(bf16[512,96]{0,1:T(8,128)(2,1)} %param.17) | copy-start | bytes 294916
  313.2 16.6 %copy-start.10 = (f32[512]{0:T(512)S(1)}, f32[512]{0:T(512)}, u32[]{:S(2)}) copy-start(f32[512]{0:T(512)} %param.18) | copy-start | bytes 6148
  314.0 15.5 %all-to-all-start.2 = ((bf16[4,3,8,768]{3,0,1,2:T(4,128)(2,1)}), bf16[4,3,8,768]{3,0,1,2:T(4,128)(2,1)S(1)}, u32[]{:S(2)}, u32[]{:S(2)}) async-start(bf16[4,3,8,768]{3,0,1,2:T(4,128)(2,1)} %copy.235), calls=%async_computation.2 | async-start | bytes 294912 | tf_op jit(solution)/shard_map/all_to_all | solution.py:177
  321.2 270.6 %all-reduce.5.cloned.1.call-start = ((), (), s32[]{:S(2)}) async-start(), calls=%async_computation.5 | async-start | bytes 2883584 | tf_op jit(solution)/shard_map/psum | solution.py:182
  321.5 8.7 %copy-start.12 = (f32[512]{0:T(512)S(1)}, f32[512]{0:T(512)}, u32[]{:S(2)}) copy-start(f32[512]{0:T(512)} %param.20) | copy-start | bytes 6148
  330.2 0.9 copy-start.6
  336.4 5.4 copy-start.1
  337.5 81.5 %all-to-all-start.3 = ((bf16[4,24,1,768]{3,0,2,1:T(4,128)(2,1)}), bf16[4,24,1,768]{3,0,2,1:T(4,128)(2,1)S(1)}, u32[]{:S(2)}, u32[]{:S(2)}) async-start(bf16[4,24,1,768]{3,0,2,1:T(4,128)(2,1)} %copy.237), calls=%async_computation.3 | async-start | bytes 294912 | tf_op jit(solution)/shard_map/all_to_all | solution.py:179
  591.8 3.9 copy-start.3
Sparse Core Ops, SparseCore 0:
  336.5 255.2 all-reduce.4
where the time goes:
time: 615 us; the launch traced here: 604 us
  waiting for transfers between devices  193 us (31%)
  loops' own time  173 us (28%)
  blocking collectives  75.9 us (12%)
  local copies, waits for them, and re-layouts  67 us (11%)
  starting transfers between devices  35.7 us (6%)
  other arithmetic  22.5 us (4%)
  matrix products  22 us (4%)
  between operations  14.8 us (2%)
    another operation x1, loops' own time, spectral_pass(): (recurrence, synthesized), blocks = lax.scan(visit_block, initial, starts)  173 us
    psum x1, waiting for transfers between devices, on_device(): lax.psum((totals[0] * grad_scale, totals[1] * grad_scale, totals[2] * gra...  172 us
    psum x1, blocking collectives, on_device(): lax.psum((totals[0] * grad_scale, totals[1] * grad_scale, totals[2] * gra...  75.9 us
    unnamed x37, local copies, waits for them, and re-layouts  28.6 us
  transfers between devices with their start and end apart: 6, of which 4 were waited for; matrix products, arithmetic and copies ran while one was open for 3% of the time, Pallas kernels for 0%

commit v1 on v0

v1 whole, which is shorter than its diff:
```python
import math

import jax
import jax.numpy as jnp
import numpy as np
from jax import lax
from jax.experimental import pallas as pl
from jax.experimental.pallas import tpu as pltpu
from jax.sharding import PartitionSpec as P

f32 = jnp.float32
bf16 = jnp.bfloat16

TRUNC = 256
NLON = 768
N_LAT = 32
N_LEV = 8
WAVES = 8
ROWS = 8
PAD = 16
USED = 12
HALF = TRUNC * WAVES
SCALE_BITS = 110
MESH = pl.DeviceIdType.MESH
VMEM = pl.BlockSpec(memory_space=pltpu.VMEM)
SMEM = pl.BlockSpec(memory_space=pltpu.SMEM)


def dft_tables():
    n = np.arange(NLON)[:, None]
    m = np.arange(TRUNC)[None, :]
    angle = 2.0 * np.pi * ((n * m) % NLON) / NLON
    table = np.concatenate([np.cos(angle), -np.sin(angle)], axis=1)
    high = table.astype(jnp.bfloat16)
    low = (table - high.astype(np.float64)).astype(jnp.bfloat16)
    return jnp.asarray(high), jnp.asarray(low)


def diagonal_table():
    index = np.arange(1, TRUNC, dtype=np.float64)
    ratios = 0.5 * np.log((2.0 * index + 1.0) / (2.0 * index))
    totals = np.concatenate([[0.0], np.cumsum(ratios)]) - 0.5 * np.log(2.0)
    return jnp.asarray(totals.astype(np.float32)[None, :])


def degree_table():
    degree = np.arange(TRUNC, dtype=np.float64)
    root = np.sqrt(np.maximum(4.0 * degree * degree - 1.0, 0.0))
    before = np.concatenate([[1.0], np.maximum(root[:-1], 1.0)])
    return jnp.asarray(np.stack([root, 1.0 / before]).astype(np.float32))


def iota(shape, axis):
    return lax.broadcasted_iota(jnp.int32, shape, axis)


def mm(a, b):
    return lax.dot_general(a, b, (((1,), (0,)), ((), ())), preferred_element_type=f32)


def mm_nt(a, b):
    return lax.dot_general(a, b, (((1,), (1,)), ((), ())), preferred_element_type=f32)


def split(value):
    high = value.astype(bf16)
    return high, (value - high.astype(f32)).astype(bf16)


def wave_onehot(order_ref):
    return (iota((TRUNC, TRUNC), 0) == order_ref[...]).astype(f32).astype(bf16)


def feature_of(column):
    lev, pair = column // PAD, column % PAD
    field = (
        (pair >= 3).astype(jnp.int32) + (pair >= 6).astype(jnp.int32) + (pair >= 9).astype(jnp.int32)
    )
    feature = field * 24 + lev * 3 + pair - field * 3
    return jnp.where(pair < USED, feature, -1)


def feature_onehot(shape, feature_axis):
    column = feature_of(iota(shape, 1 - feature_axis))
    return (iota(shape, feature_axis) == column).astype(f32).astype(bf16)


def take_rows(rows, source, target):
    for c in range(NLON // 128):
        rows[96 * c : 96 * (c + 1), :] = source[:, 128 * c : 128 * (c + 1)].astype(f32)
        for a in range(ROWS):
            picked = rows[pl.ds(96 * c + a, USED, stride=ROWS), :]
            target[PAD * a : PAD * a + USED, 128 * c : 128 * (c + 1)] = picked


def forward_kernel(
    x_ref, ct_ref, high_ref, low_ref, order_ref, lat_ref, four_ref, up_ref, rows, xs, fs
):
    lat = lax.axis_index("lat")
    xs[...] = jnp.zeros_like(xs)
    take_rows(rows, ct_ref, xs)
    for a in range(ROWS):
        up_ref[a] = xs[PAD * a : PAD * (a + 1), :].astype(bf16)
    take_rows(rows, x_ref, xs)
    xh, xl = split(xs[...])
    modes = mm(xh, high_ref[...]) + mm(xl, high_ref[...]) + mm(xh, low_ref[...])
    theta = (math.pi / 256.0) * (lat_ref[...].astype(f32) + 0.5)
    weight = (math.pi / 256.0 / NLON) * jnp.sin(theta)
    row = iota((ROWS * PAD, 256), 0) // PAD + lat * ROWS
    picked = jnp.where(iota((ROWS * PAD, 256), 1) == row, weight, 0.0)
    modes = (modes * jnp.sum(picked, axis=1, keepdims=True)).astype(bf16)
    onehot = wave_onehot(order_ref)
    for k in range(2):
        ordered = mm(modes[:, k * 256 : (k + 1) * 256], onehot)
        fs[:, 8 * k : 8 * (k + 1), :] = ordered.T.reshape(N_LAT, 8, 128)
    four_ref[...] = fs[...].astype(bf16)


def legendre_kernel(
    four_ref, order_ref, lat_ref, diag_ref, deg_ref, damp_ref, spec_ref, out_ref, table, rs, so
):
    lat = lax.axis_index("lat")
    lane = iota((WAVES, 256), 1)
    mine = lane == lat * WAVES + iota((WAVES, 256), 0)
    order = order_ref[...].astype(f32)
    wave = jnp.sum(jnp.where(mine, order, 0.0), axis=1, keepdims=True)
    diag_log = jnp.sum(
        jnp.where(lane.astype(f32) == wave, diag_ref[...], 0.0), axis=1, keepdims=True
    )
    source = (iota((256, 256), 1) % N_LAT) * ROWS + iota((256, 256), 1) // N_LAT
    reorder = (iota((256, 256), 0) == source).astype(f32).astype(bf16)
    lat_row = jnp.broadcast_to(lat_ref[...].astype(f32), (8, 256)).astype(bf16)
    theta = (math.pi / 256.0) * (mm(lat_row, reorder) + 0.5)
    cosine = jnp.cos(theta)
    start = jnp.exp(diag_log + wave * jnp.log(jnp.sin(theta)) + SCALE_BITS * math.log(2.0))
    wave128 = jnp.broadcast_to(wave, (WAVES, 128))
    square = wave128 * wave128
    descale = 2.0**-SCALE_BITS

    def step(degree, carried):
        latest, before, root_before = carried
        value = degree.astype(f32)
        gap = value * value - square
        safe = jnp.maximum(gap, 1.0)
        inverse = lax.rsqrt(safe)
        inverse = inverse * (1.5 - 0.5 * safe * inverse * inverse)
        root = jnp.maximum(gap, 0.0) * inverse
        upper = inverse * deg_ref[0, degree]
        lower = upper * root_before * deg_ref[1, degree]
        upper2 = jnp.concatenate([upper, upper], axis=1)
        lower2 = jnp.concatenate([lower, lower], axis=1)
        first = jnp.where(wave == value, start, 0.0)
        newest = (upper2 * cosine) * latest + (first - lower2 * before)
        scaled = newest * descale
        at = pl.multiple_of(degree * WAVES, WAVES)
        table[pl.ds(at, WAVES), :] = scaled[:, :128]
        table[pl.ds(at + HALF, WAVES), :] = scaled[:, 128:]
        return newest, latest, root

    table[0:WAVES, :] = jnp.zeros((WAVES, 128), f32)
    half = table[0:WAVES, :]
    zero = jnp.concatenate([half, half], axis=1)
    lax.fori_loop(0, TRUNC, step, (zero, zero, half), unroll=8)

    pair = iota((PAD, 256), 0)
    damping = jnp.zeros((PAD, 256), f32)
    for i in range(USED):
        damping = jnp.where(pair == i, damp_ref[i // 3, i % 3], damping)
    degree = iota((PAD, 256), 1).astype(f32)
    ratio = degree * (degree + 1.0) * (1.0 / (TRUNC * (TRUNC - 1.0)))
    response = 1.0 / (1.0 + damping * ratio * ratio)
    response = jnp.concatenate([response, response], axis=0)

    for i in range(N_LAT):
        rs[i] = four_ref[i].astype(f32)
    flat = rs.reshape(N_LAT * PAD, 128)
    turned = []
    for q in range(4):
        block = jnp.concatenate(
            [flat[pl.ds(4 * q + i, N_LAT, stride=PAD), :] for i in range(4)], axis=0
        )
        turned.append(block.T)

    def rows_of(kj):
        piece = turned[kj // 4]
        low = 32 * (kj % 4)
        return jnp.concatenate(
            [piece[PAD * a : PAD * (a + 1), low : low + 32] for a in range(ROWS)], axis=1
        )

    made = [None] * 16
    for j in range(WAVES):
        field = jnp.concatenate([rows_of(j), rows_of(8 + j)], axis=0).astype(bf16)
        left = table[pl.ds(j, TRUNC, stride=WAVES), :]
        right = table[pl.ds(HALF + j, TRUNC, stride=WAVES), :]
        high, low = split(jnp.concatenate([left, right], axis=1))
        coeffs = (mm_nt(field, high) + mm_nt(field, low)) * response
        for k in range(2):
            for f in range(4):
                at = PAD * k + 3 * f
                spec_ref[j, k, f] = coeffs[at : at + 3, :]
        ch, cl = split(coeffs)
        grid = mm(ch, high) + mm(cl, high) + mm(ch, low)
        made[j] = grid[:PAD]
        made[8 + j] = grid[PAD:]
    flat_out = so.reshape(N_LAT * PAD, 128)
    for q in range(4):
        block = jnp.concatenate(
            [
                jnp.concatenate(
                    [made[4 * q + i][:, 32 * a : 32 * (a + 1)] for i in range(4)], axis=1
                )
                for a in range(ROWS)
            ],
            axis=0,
        )
        back = block.T
        for i in range(4):
            flat_out[pl.ds(4 * q + i, N_LAT, stride=PAD), :] = back[32 * i : 32 * (i + 1)]
    out_ref[...] = so[...]


def inverse_kernel(syn_ref, high_ref, low_ref, order_ref, scale_ref, filt_ref, in_ref, turn):
    lev = lax.axis_index("lev")
    onehot = wave_onehot(order_ref)
    factor = jnp.where(iota((TRUNC, 128), 0) == 0, 1.0, 2.0)
    parts = []
    for k in range(2):
        part_high, part_low = split(syn_ref[:, 8 * k : 8 * (k + 1), :].reshape(TRUNC, 128))
        parts.append(((mm(onehot, part_high) + mm(onehot, part_low)) * factor).T)
    mh, ml = split(jnp.concatenate(parts, axis=1))
    rows = mm_nt(mh, high_ref[...]) + mm_nt(ml, high_ref[...]) + mm_nt(mh, low_ref[...])
    pair = iota((PAD, NLON), 0)
    scale = jnp.zeros((PAD, NLON), f32)
    for i in range(USED):
        scale = jnp.where(pair == i, scale_ref[i // 3, lev * 3 + i % 3], scale)
    for a in range(ROWS):
        piece = rows[PAD * a : PAD * (a + 1), :]
        for c in range(NLON // 128):
            turn[pl.ds(96 * c + a, USED, stride=ROWS), :] = piece[:USED, 128 * c : 128 * (c + 1)]
        in_ref[a] = (piece * scale).astype(bf16)
    for c in range(NLON // 128):
        filt_ref[:, 128 * c : 128 * (c + 1)] = turn[96 * c : 96 * (c + 1), :]


def network_kernel(
    in_ref, up_ref, win_ref, bin_ref, wmid_ref, bmid_ref, wout_ref, tend_ref, grad_ref,
    win_s, wout_s, woutT_s, wmidT_s, bin_s, bmid_s, in_s, up_s, tend_s, gin, gmid, gout, gbm,
):
    win_s[...] = mm(win_ref[...], feature_onehot((96, 128), 0)).astype(bf16)
    wout = mm(feature_onehot((128, 96), 1), wout_ref[...])
    wout_s[...] = wout.astype(bf16)
    woutT_s[...] = wout.T.astype(bf16)
    wmidT_s[...] = wmid_ref[...].astype(f32).T.astype(bf16)
    bin_s[...] = jnp.broadcast_to(bin_ref[...], (128, 512)).T
    bmid_s[...] = jnp.broadcast_to(bmid_ref[...], (128, 512)).T
    inputs = in_ref[...].reshape(128, NLON)
    in_s[...] = jnp.where(iota((128, NLON), 0) == USED, 1.0, inputs.astype(f32)).astype(bf16)
    up_s[...] = up_ref[...].reshape(128, NLON)
    gin[...] = jnp.zeros_like(gin)
    gmid[...] = jnp.zeros_like(gmid)
    gout[...] = jnp.zeros_like(gout)
    gbm[...] = jnp.zeros_like(gbm)

    def activation(value):
        z = 0.5 + 0.5 * jnp.tanh(0.5 * value)
        return value * z, z * (1.0 + value * (1.0 - z))

    def chunk(c, _):
        cols = pl.ds(pl.multiple_of(c * 256, 256), 256)
        inp, up = in_s[:, cols], up_s[:, cols]
        b_in = jnp.concatenate([bin_s[...], bin_s[...]], axis=1)
        h_in, slope_in = activation(mm(win_s[...], inp) + b_in)
        h_in = h_in.astype(bf16)
        b_mid = jnp.concatenate([bmid_s[...], bmid_s[...]], axis=1)
        h_mid, slope_mid = activation(mm(wmid_ref[...], h_in) + b_mid)
        h_mid = h_mid.astype(bf16)
        tend_s[:, cols] = mm(wout_s[...], h_mid).astype(bf16)
        gout[...] += mm_nt(h_mid, up)
        d_mid = (mm(woutT_s[...], up) * slope_mid).astype(bf16)
        gmid[...] += mm_nt(d_mid, h_in)
        wide = d_mid.astype(f32)
        gbm[...] += wide[:, :128] + wide[:, 128:]
        d_in = (mm(wmidT_s[...], d_mid) * slope_in).astype(bf16)
        gin[...] += mm_nt(d_in, inp)
        return 0

    lax.fori_loop(0, 3, chunk, 0)
    tend_ref[...] = tend_s[...].reshape(N_LEV, PAD, NLON)
    norm = 1.0 / math.sqrt(256 * NLON)
    bias = jnp.sum(gbm[...], axis=1, keepdims=True)
    last = jnp.where(iota((512, 128), 1) == USED, bias, gout[...])
    grad_ref[:, :, 0:128] = (gin[...] * norm).astype(bf16).reshape(N_LAT, 16, 128)
    grad_ref[:, :, 128:640] = (gmid[...] * norm).astype(bf16).reshape(N_LAT, 16, 512)
    grad_ref[:, :, 640:768] = (last * norm).astype(bf16).reshape(N_LAT, 16, 128)


def finish_kernel(
    filt_ref, tend_ref, grad_ref, state_ref, gin_ref, gbin_ref, gmid_ref, gbmid_ref, gout_ref, turn
):
    for a in range(ROWS):
        piece = tend_ref[a].astype(f32)
        for c in range(NLON // 128):
            turn[pl.ds(96 * c + a, USED, stride=ROWS), :] = piece[:USED, 128 * c : 128 * (c + 1)]
    for c in range(NLON // 128):
        cols = slice(128 * c, 128 * (c + 1))
        state_ref[:, cols] = filt_ref[:, cols] + turn[96 * c : 96 * (c + 1), :]
    total = grad_ref[...].reshape(512, NLON)
    first, last = total[:, :128], total[:, 640:]
    gin_ref[...] = mm(first, feature_onehot((128, 96), 1))
    gout_ref[...] = mm_nt(feature_onehot((96, 128), 0), last)
    gmid_ref[...] = total[:, 128:640].astype(f32)
    pick = (iota((8, 128), 1) == USED).astype(f32).astype(bf16)
    gbin_ref[...] = mm_nt(pick, first)[:1]
    gbmid_ref[...] = mm_nt(pick, last)[:1]


def greet(axes):
    barrier = pltpu.get_barrier_semaphore()
    for axis, size in axes:
        me = lax.axis_index(axis)

        def signal(d, _):
            peer = lax.rem(me + d, size)
            pl.semaphore_signal(barrier, inc=1, device_id={axis: peer}, device_id_type=MESH)
            return 0

        lax.fori_loop(1, size, signal, 0)
    pl.semaphore_wait(barrier, sum(size - 1 for _, size in axes))


def scatter(axis, size, source, landing, send, recv):
    me = lax.axis_index(axis)

    def copy(d):
        peer = lax.rem(me + d, size)
        return pltpu.make_async_remote_copy(
            src_ref=source(peer), dst_ref=landing.at[me], send_sem=send.at[d],
            recv_sem=recv.at[d], device_id={axis: peer}, device_id_type=MESH,
        )

    def start(d, _):
        copy(d).start()
        return 0

    def wait(d, _):
        copy(d).wait()
        return 0

    lax.fori_loop(1, size, start, 0)
    return lambda: lax.fori_loop(1, size, wait, 0)


def exchange_two_kernel(four, up, four_out, up_out, s0, r0, s1, r1):
    greet((("lat", N_LAT), ("lev", N_LEV)))
    wait_up = scatter("lev", N_LEV, lambda p: up.at[p], up_out, s1, r1)
    wait_four = scatter("lat", N_LAT, lambda p: four.at[p], four_out, s0, r0)
    lat, lev = lax.axis_index("lat"), lax.axis_index("lev")
    four_out[lat] = four[lat]
    up_out[lev] = up[lev]
    wait_four()
    wait_up()


def exchange_kernel(axis, size, block, block_out, send, recv):
    greet(((axis, size),))
    wait = scatter(axis, size, lambda p: block.at[p], block_out, send, recv)
    me = lax.axis_index(axis)
    block_out[me] = block[me]
    wait()


def reduce_kernel(tend, grad, tend_out, total, parts, piece, pieces, done, s0, r0, s1, r1, s2, r2, s3, r3):
    greet((("lat", N_LAT), ("lev", N_LEV)))
    lat, lev = lax.axis_index("lat"), lax.axis_index("lev")
    wait_tend = scatter("lev", N_LEV, lambda p: tend.at[p], tend_out, s0, r0)
    wait_parts = scatter("lat", N_LAT, lambda p: grad.at[p], parts, s1, r1)
    tend_out[lev] = tend[lev]
    parts[lat] = grad[lat]
    wait_parts()

    def add(ref):
        def body(i, acc):
            return acc + ref[i].astype(f32)

        return body

    piece[...] = lax.fori_loop(1, N_LAT, add(parts), parts[0].astype(f32)).astype(bf16)
    wait_pieces = scatter("lev", N_LEV, lambda p: piece, pieces, s2, r2)
    pieces[lev] = piece[...]
    wait_pieces()
    done[...] = lax.fori_loop(1, N_LEV, add(pieces), pieces[0].astype(f32)).astype(bf16)
    wait_total = scatter("lat", N_LAT, lambda p: done, total, s3, r3)
    total[lat] = done[...]
    wait_total()
    wait_tend()


def like(shape, dtype):
    return jax.ShapeDtypeStruct(shape, dtype)


def local(kernel, out_shape, scratch, in_specs, name):
    return pl.pallas_call(
        kernel,
        out_shape=out_shape,
        in_specs=in_specs,
        out_specs=jax.tree.map(lambda _: VMEM, out_shape),
        scratch_shapes=scratch,
        name=name,
    )


def remote(kernel, out_shape, scratch, count, number, name):
    return pl.pallas_call(
        kernel,
        out_shape=out_shape,
        in_specs=[VMEM] * count,
        out_specs=jax.tree.map(lambda _: VMEM, out_shape),
        scratch_shapes=scratch,
        compiler_params=pltpu.CompilerParams(collective_id=number, has_side_effects=True),
        name=name,
    )


def sems(count):
    return [pltpu.SemaphoreType.DMA((count,)), pltpu.SemaphoreType.DMA((count,))]


def on_device(
    prognostic, cotangent, damping, in_scale, w_in, b_in, w_mid, b_mid, w_out, wave_order, lat_order
):
    high, low = dft_tables()
    order = wave_order.reshape(1, TRUNC)
    lats = lat_order.reshape(1, 256)
    rows96 = ROWS * USED
    waves_block = like((N_LAT, PAD, 128), bf16)
    wide_block = like((N_LAT, PAD, 128), f32)
    rows_block = like((N_LEV, PAD, NLON), bf16)

    four, up = local(
        forward_kernel, (waves_block, rows_block),
        [pltpu.VMEM((576, 128), f32), pltpu.VMEM((128, NLON), f32), pltpu.VMEM((N_LAT, PAD, 128), f32)],
        [VMEM] * 6, "forward",
    )(prognostic.reshape(rows96, NLON), cotangent.reshape(rows96, NLON), high, low, order, lats)

    four, up = remote(
        exchange_two_kernel, (waves_block, rows_block), sems(N_LAT) + sems(N_LEV), 2, 0, "exchange_a"
    )(four, up)

    spectral, synth = local(
        legendre_kernel, (like((WAVES, 2, 4, 3, TRUNC), f32), wide_block),
        [pltpu.VMEM((2 * HALF, 128), f32), pltpu.VMEM((N_LAT, PAD, 128), f32),
         pltpu.VMEM((N_LAT, PAD, 128), f32)],
        [VMEM] * 4 + [SMEM] * 2, "legendre",
    )(four, order, lats, diagonal_table(), degree_table(), damping)

    synth = remote(
        lambda *refs: exchange_kernel("lat", N_LAT, *refs), wide_block, sems(N_LAT), 1, 1, "exchange_b"
    )(synth)

    filtered, inputs = local(
        inverse_kernel, (like((rows96, NLON), f32), rows_block),
        [pltpu.VMEM((576, 128), f32)], [VMEM] * 4 + [SMEM], "inverse",
    )(synth, high, low, order, in_scale)

    inputs = remote(
        lambda *refs: exchange_kernel("lev", N_LEV, *refs), rows_block, sems(N_LEV), 1, 2, "exchange_c"
    )(inputs)

    grad_block = like((N_LAT, 16, NLON), bf16)
    tendency, grads = local(
        network_kernel, (rows_block, grad_block),
        [pltpu.VMEM((512, 128), bf16), pltpu.VMEM((128, 512), bf16), pltpu.VMEM((512, 128), bf16),
         pltpu.VMEM((512, 512), bf16), pltpu.VMEM((512, 128), f32), pltpu.VMEM((512, 128), f32),
         pltpu.VMEM((128, NLON), bf16), pltpu.VMEM((128, NLON), bf16), pltpu.VMEM((128, NLON), bf16),
         pltpu.VMEM((512, 128), f32), pltpu.VMEM((512, 512), f32), pltpu.VMEM((512, 128), f32),
         pltpu.VMEM((512, 128), f32)],
        [VMEM] * 7, "network",
    )(inputs, up, w_in, b_in.reshape(1, 512), w_mid, b_mid.reshape(1, 512), w_out)

    tendency, grads = remote(
        reduce_kernel, (rows_block, grad_block),
        [pltpu.VMEM((N_LAT, 16, NLON), bf16), pltpu.VMEM((16, NLON), bf16),
         pltpu.VMEM((N_LEV, 16, NLON), bf16), pltpu.VMEM((16, NLON), bf16)]
        + sems(N_LEV) + sems(N_LAT) + sems(N_LEV) + sems(N_LAT),
        2, 3, "exchange_d",
    )(tendency, grads)

    state, gin, gbin, gmid, gbmid, gout = local(
        finish_kernel,
        (like((rows96, NLON), f32), like((512, 96), f32), like((1, 512), f32),
         like((512, 512), f32), like((1, 512), f32), like((96, 512), f32)),
        [pltpu.VMEM((576, 128), f32)], [VMEM] * 3, "finish",
    )(filtered, tendency, grads)
    return (
        state.reshape(prognostic.shape), spectral, gin, gbin.reshape(512), gmid, gbmid.reshape(512), gout,
    )


def solution(mesh):
    return jax.shard_map(
        on_device,
        mesh=mesh,
        in_specs=(
            P(None, "lev", "lat", None),
            P(None, "lev", "lat", None),
            P(None, "lev"),
            P(),
            P(),
            P(),
            P(),
            P(),
            P(),
            P(),
            P(),
        ),
        out_specs=(
            P(None, "lev", "lat", None),
            P("lat", None, None, "lev", None),
            P(),
            P(),
            P(),
            P(),
            P(),
        ),
        check_vma=False,
    )
```

time: 615 us -> 116 us (0.19); the launches traced: 604 us -> 115 us
  waiting for transfers between devices: 193 us -> 0 us
  loops' own time: 173 us -> 0 us
  Pallas kernels: 0 us -> 111 us
  blocking collectives: 75.9 us -> 0 us
  local copies, waits for them, and re-layouts: 67 us -> 4.14 us
  starting transfers between devices: 35.7 us -> 0 us
  other arithmetic: 22.5 us -> 0 us
  matrix products: 22 us -> 0 us
  between operations: 14.8 us -> 0.68 us
    another operation x1 -> x0, loops' own time: 173 us -> none  [spectral_pass(): (recurrence, synthesized), blocks = lax.scan(visit_block, initial, starts)]
    psum x1 -> x0, waiting for transfers between devices: 172 us -> none  [on_device(): lax.psum((totals[0] * grad_scale, totals[1] * grad_scale, totals[2] * gra...]
    pallas_call x0 -> x9, Pallas kernels: none -> 111 us  [the longest x1 41 us: on_device(): remote(reduce_kernel, (rows_block, grad_block), [pltpu.VMEM((N_LAT, 16, N...]
    psum x1 -> x0, blocking collectives: 75.9 us -> none  [on_device(): lax.psum((totals[0] * grad_scale, totals[1] * grad_scale, totals[2] * gra...]
    all_to_all x5 -> x0, starting transfers between devices: 35.4 us -> none  [the longest x1 10.7 us: on_device(): lax.all_to_all(cotangent, 'lev', split_axis=2, concat_axis=1, tiled=True)]
    unnamed x37 -> x5, local copies, waits for them, and re-layouts: 28.6 us -> 4.14 us
    dot_general x26 -> x0, matrix products: 22 us -> none  [the longest x8 8.93 us: visit_block(): jnp.einsum('jbn,jkfen->jkfeb', legendre_table, weighted, precision=lax.Pr...]
    all_to_all x5 -> x0, waiting for transfers between devices: 21.3 us -> none  [the longest x1 7.81 us: on_device(): lax.all_to_all(local_inputs, 'lev', split_axis=2, concat_axis=1, tiled=True)]
  transfers between devices with their start and end apart: 6 -> 0, of which waited for: 4 -> 0; matrix products, arithmetic and copies ran while one was open for 3% -> 0% of each run, Pallas kernels for 0% -> 0%
where the time goes in v1:
time: 116 us; the launch traced here: 115 us
  Pallas kernels  111 us (96%)
  local copies, waits for them, and re-layouts  4.14 us (4%)
    pallas_call x1, Pallas kernels, on_device(): remote(reduce_kernel, (rows_block, grad_block), [pltpu.VMEM((N_LAT, 16, N...  41 us
    pallas_call x1, Pallas kernels, on_device(): remote(exchange_two_kernel, (waves_block, rows_block), sems(N_LAT) + sems...  22.1 us
    pallas_call x1, Pallas kernels, on_device(): remote(lambda *refs: exchange_kernel('lev', N_LEV, *refs), rows_block, se...  13.9 us
    pallas_call x1, Pallas kernels, on_device(): remote(lambda *refs: exchange_kernel('lat', N_LAT, *refs), wide_block, se...  10.4 us
    pallas_call x1, Pallas kernels, on_device(): local(network_kernel, (rows_block, grad_block), [pltpu.VMEM((512, 128), b...  7.3 us
    pallas_call x1, Pallas kernels, on_device(): local(legendre_kernel, (like((WAVES, 2, 4, 3, TRUNC), f32), wide_block),...  6.69 us
    unnamed x5, local copies, waits for them, and re-layouts  4.14 us
    pallas_call x1, Pallas kernels, on_device(): local(inverse_kernel, (like((rows96, NLON), f32), rows_block), [pltpu.VME...  3.46 us

profile of v1, /device:TPU:1, one launch (start us, length us, event | category | flops | bytes accessed | tf_op | source)
XLA Modules:
  0.0 115.4 jit_solution(13918765384497297122)
XLA Ops:
  0.6 1.7 %copy.22.win_ref = bf16[512,96]{1,0:T(8,128)(2,1)} copy(bf16[512,96]{0,1:T(8,128)(2,1)} %param.19) | data formatting | bytes 196608 | tf_op args[4]
  2.3 3.0 %forward.1 = (bf16[32,16,128]{2,1,0:T(8,128)(2,1)}, bf16[8,16,768]{2,1,0:T(8,128)(2,1)}) custom-call(f32[96,768]{1,0:T(8,128)} %bitcast.9, bf16[96,768]{1,0:T(8,128)(2,1)} %bitcast.10, bf16[768,512]{1,0:T(8,128)(2,1)} %constant.8.clone.high_ref, bf16[768,512]{1,0:T(8,128)(2,1)} %constant.9.clone.low_ref, s32[1,256]{1,0:T(1,128)} %bitcast.11, s32[1,256]{1,0:T(1,128)} %bitcast.14), custom_call_target="tpu_custom_call" | custom-call | tf_op jit(solution)/shard_map/forward/pallas_call | solution.py:441
  5.3 22.1 %exchange_a.1 = (bf16[32,16,128]{2,1,0:T(8,128)(2,1)}, bf16[8,16,768]{2,1,0:T(8,128)(2,1)}) custom-call(bf16[32,16,128]{2,1,0:T(8,128)(2,1)} %get-tuple-element.25.four, bf16[8,16,768]{2,1,0:T(8,128)(2,1)} %get-tuple-element.26.up), custom_call_target="tpu_custom_call" | custom-call | tf_op jit(solution)/shard_map/exchange_a/pallas_call | solution.py:447
  27.4 6.7 %legendre.1 = (f32[8,2,4,3,256]{4,3,2,1,0:T(4,128)}, f32[32,16,128]{2,1,0:T(8,128)}) custom-call(bf16[32,16,128]{2,1,0:T(8,128)(2,1)} %get-tuple-element.27.four_ref, s32[1,256]{1,0:T(1,128)} %bitcast.12, s32[1,256]{1,0:T(1,128)} %bitcast.15, f32[1,256]{1,0:T(1,128)} %constant.10.clone.diag_ref, f32[2,256]{1,0:T(2,128)} %constant.11.clone.deg_ref, ...), custom_call_target="tpu_custom_call" | custom-call | tf_op jit(solution)/shard_map/legendre/pallas_call | solution.py:451
  34.1 0.0 copy-start
  34.1 10.4 %exchange_b.1.syn_ref = f32[32,16,128]{2,1,0:T(8,128)} custom-call(f32[32,16,128]{2,1,0:T(8,128)} %get-tuple-element.28.refs_0_), custom_call_target="tpu_custom_call" | custom-call | tf_op jit(solution)/shard_map/exchange_b/pallas_call | solution.py:458
  44.5 0.0 copy-done
  44.5 0.7 copy.23
  45.3 3.5 %inverse.1 = (f32[96,768]{1,0:T(8,128)}, bf16[8,16,768]{2,1,0:T(8,128)(2,1)}) custom-call(f32[32,16,128]{2,1,0:T(8,128)} %exchange_b.1.syn_ref, bf16[768,512]{1,0:T(8,128)(2,1)} %constant.8.clone.high_ref, bf16[768,512]{1,0:T(8,128)(2,1)} %constant.9.clone.low_ref, s32[1,256]{1,0:T(1,128)} %bitcast.13, f32[4,24]{1,0:T(4,128)} %scale_ref.1), custom_call_target="tpu_custom_call" | custom-call | tf_op jit(solution)/shard_map/inverse/pallas_call | solution.py:462
  48.7 13.9 %exchange_c.1.in_ref = bf16[8,16,768]{2,1,0:T(8,128)(2,1)} custom-call(bf16[8,16,768]{2,1,0:T(8,128)(2,1)} %get-tuple-element.30.refs_0_), custom_call_target="tpu_custom_call" | custom-call | tf_op jit(solution)/shard_map/exchange_c/pallas_call | solution.py:467
  62.6 7.3 %network.1 = (bf16[8,16,768]{2,1,0:T(8,128)(2,1)}, bf16[32,16,768]{2,1,0:T(8,128)(2,1)}) custom-call(bf16[8,16,768]{2,1,0:T(8,128)(2,1)} %exchange_c.1.in_ref, bf16[8,16,768]{2,1,0:T(8,128)(2,1)} %get-tuple-element.31.up_ref, bf16[512,96]{1,0:T(8,128)(2,1)} %copy.22.win_ref, f32[1,512]{1,0:T(1,128)} %bitcast.16, bf16[512,512]{1,0:T(8,128)(2,1)} %wmid_ref.1, ...), custom_call_target="tpu_custom_call" | custom-call | tf_op jit(solution)/shard_map/network/pallas_call | solution.py:472
  69.9 41.0 %exchange_d.1 = (bf16[8,16,768]{2,1,0:T(8,128)(2,1)}, bf16[32,16,768]{2,1,0:T(8,128)(2,1)}) custom-call(bf16[8,16,768]{2,1,0:T(8,128)(2,1)} %get-tuple-element.32.tend, bf16[32,16,768]{2,1,0:T(8,128)(2,1)} %get-tuple-element.33.grad), custom_call_target="tpu_custom_call" | custom-call | tf_op jit(solution)/shard_map/exchange_d/pallas_call | solution.py:482
  111.0 2.7 %finish.1 = (f32[96,768]{1,0:T(8,128)}, f32[512,96]{1,0:T(8,128)}, f32[1,512]{1,0:T(1,128)}, f32[512,512]{1,0:T(8,128)}, f32[1,512]{1,0:T(1,128)}, /*index=5*/f32[96,512]{1,0:T(8,128)}) custom-call(f32[96,768]{1,0:T(8,128)} %get-tuple-element.29.filt_ref, bf16[8,16,768]{2,1,0:T(8,128)(2,1)} %get-tuple-element.34.tend_ref, ...), custom_call_target="tpu_custom_call" | custom-call | tf_op jit(solution)/shard_map/finish/pallas_call | solution.py:490
  113.7 1.8 %copy.24 = f32[512,96]{0,1:T(8,128)} copy(f32[512,96]{1,0:T(8,128)} %get-tuple-element.45) | data formatting | bytes 393216
Async XLA Ops:
  34.1 10.4 %copy-start = (f32[8,2,4,3,256]{4,3,2,1,0:T(4,128)S(1)}, f32[8,2,4,3,256]{4,3,2,1,0:T(4,128)}, u32[]{:S(2)}) copy-start(f32[8,2,4,3,256]{4,3,2,1,0:T(4,128)} %get-tuple-element.44) | copy-start | bytes 589828

commit v2 on v1

v2 whole, which is shorter than its diff:
```python
import math

import jax
import jax.numpy as jnp
import numpy as np
from jax import lax
from jax.experimental import pallas as pl
from jax.experimental.pallas import tpu as pltpu
from jax.sharding import PartitionSpec as P

f32 = jnp.float32
bf16 = jnp.bfloat16

TRUNC = 256
NLON = 768
N_LAT = 32
N_LEV = 8
WAVES = 8
ROWS = 8
PAD = 16
USED = 12
HALF = TRUNC * WAVES
SCALE_BITS = 110
MESH = pl.DeviceIdType.MESH
VMEM = pl.BlockSpec(memory_space=pltpu.VMEM)
SMEM = pl.BlockSpec(memory_space=pltpu.SMEM)


def dft_tables():
    n = np.arange(NLON)[:, None]
    m = np.arange(TRUNC)[None, :]
    angle = 2.0 * np.pi * ((n * m) % NLON) / NLON
    table = np.concatenate([np.cos(angle), -np.sin(angle)], axis=1)
    high = table.astype(jnp.bfloat16)
    low = (table - high.astype(np.float64)).astype(jnp.bfloat16)
    return jnp.asarray(high), jnp.asarray(low)


def diagonal_table():
    index = np.arange(1, TRUNC, dtype=np.float64)
    ratios = 0.5 * np.log((2.0 * index + 1.0) / (2.0 * index))
    totals = np.concatenate([[0.0], np.cumsum(ratios)]) - 0.5 * np.log(2.0)
    return jnp.asarray(totals.astype(np.float32)[None, :])


def degree_table():
    degree = np.arange(TRUNC, dtype=np.float64)
    root = np.sqrt(np.maximum(4.0 * degree * degree - 1.0, 0.0))
    before = np.concatenate([[1.0], np.maximum(root[:-1], 1.0)])
    return jnp.asarray(np.stack([root, 1.0 / before]).astype(np.float32))


def iota(shape, axis):
    return lax.broadcasted_iota(jnp.int32, shape, axis)


def mm(a, b):
    return lax.dot_general(a, b, (((1,), (0,)), ((), ())), preferred_element_type=f32)


def mm_nt(a, b):
    return lax.dot_general(a, b, (((1,), (1,)), ((), ())), preferred_element_type=f32)


def split(value):
    high = value.astype(bf16)
    return high, (value - high.astype(f32)).astype(bf16)


def wave_onehot(order_ref):
    return (iota((TRUNC, TRUNC), 0) == order_ref[...]).astype(f32).astype(bf16)


def feature_of(column):
    lev, pair = column // PAD, column % PAD
    field = (
        (pair >= 3).astype(jnp.int32) + (pair >= 6).astype(jnp.int32) + (pair >= 9).astype(jnp.int32)
    )
    feature = field * 24 + lev * 3 + pair - field * 3
    return jnp.where(pair < USED, feature, -1)


def feature_onehot(shape, feature_axis):
    column = feature_of(iota(shape, 1 - feature_axis))
    return (iota(shape, feature_axis) == column).astype(f32).astype(bf16)


def take_rows(rows, source, target):
    for c in range(NLON // 128):
        rows[96 * c : 96 * (c + 1), :] = source[:, 128 * c : 128 * (c + 1)].astype(f32)
        for a in range(ROWS):
            picked = rows[pl.ds(96 * c + a, USED, stride=ROWS), :]
            target[PAD * a : PAD * a + USED, 128 * c : 128 * (c + 1)] = picked


def forward(x_ref, high_ref, low_ref, order_ref, lat_ref, rows, xs, fs, four_ref, lat):
    take_rows(rows, x_ref, xs)
    xh, xl = split(xs[...])
    modes = mm(xh, high_ref[...]) + mm(xl, high_ref[...]) + mm(xh, low_ref[...])
    theta = (math.pi / 256.0) * (lat_ref[...].astype(f32) + 0.5)
    weight = (math.pi / 256.0 / NLON) * jnp.sin(theta)
    row = iota((ROWS * PAD, 256), 0) // PAD + lat * ROWS
    picked = jnp.where(iota((ROWS * PAD, 256), 1) == row, weight, 0.0)
    modes = (modes * jnp.sum(picked, axis=1, keepdims=True)).astype(bf16)
    onehot = wave_onehot(order_ref)
    for k in range(2):
        ordered = mm(modes[:, k * 256 : (k + 1) * 256], onehot)
        fs[:, 8 * k : 8 * (k + 1), :] = ordered.T.reshape(N_LAT, 8, 128)
    four_ref[...] = fs[...].astype(bf16)


def legendre_table(order_ref, lat_ref, diag_ref, deg_ref, table, lat):
    lane = iota((WAVES, 256), 1)
    mine = lane == lat * WAVES + iota((WAVES, 256), 0)
    order = order_ref[...].astype(f32)
    wave = jnp.sum(jnp.where(mine, order, 0.0), axis=1, keepdims=True)
    diag_log = jnp.sum(
        jnp.where(lane.astype(f32) == wave, diag_ref[...], 0.0), axis=1, keepdims=True
    )
    source = (iota((256, 256), 1) % N_LAT) * ROWS + iota((256, 256), 1) // N_LAT
    reorder = (iota((256, 256), 0) == source).astype(f32).astype(bf16)
    lat_row = jnp.broadcast_to(lat_ref[...].astype(f32), (8, 256)).astype(bf16)
    theta = (math.pi / 256.0) * (mm(lat_row, reorder) + 0.5)
    cosine = jnp.cos(theta)
    start = jnp.exp(diag_log + wave * jnp.log(jnp.sin(theta)) + SCALE_BITS * math.log(2.0))
    wave128 = jnp.broadcast_to(wave, (WAVES, 128))
    square = wave128 * wave128
    descale = 2.0**-SCALE_BITS

    def step(degree, carried):
        latest, before, root_before = carried
        value = degree.astype(f32)
        gap = value * value - square
        safe = jnp.maximum(gap, 1.0)
        inverse = lax.rsqrt(safe)
        inverse = inverse * (1.5 - 0.5 * safe * inverse * inverse)
        root = jnp.maximum(gap, 0.0) * inverse
        upper = inverse * deg_ref[0, degree]
        lower = upper * root_before * deg_ref[1, degree]
        upper2 = jnp.concatenate([upper, upper], axis=1)
        lower2 = jnp.concatenate([lower, lower], axis=1)
        first = jnp.where(wave == value, start, 0.0)
        newest = (upper2 * cosine) * latest + (first - lower2 * before)
        scaled = newest * descale
        at = pl.multiple_of(degree * WAVES, WAVES)
        table[pl.ds(at, WAVES), :] = scaled[:, :128]
        table[pl.ds(at + HALF, WAVES), :] = scaled[:, 128:]
        return newest, latest, root

    table[0:WAVES, :] = jnp.zeros((WAVES, 128), f32)
    half = table[0:WAVES, :]
    zero = jnp.concatenate([half, half], axis=1)
    lax.fori_loop(0, TRUNC, step, (zero, zero, half), unroll=8)


def analysis(four_ref, damp_ref, spec_ref, table, rs, so):
    pair = iota((PAD, 256), 0)
    damping = jnp.zeros((PAD, 256), f32)
    for i in range(USED):
        damping = jnp.where(pair == i, damp_ref[i // 3, i % 3], damping)
    degree = iota((PAD, 256), 1).astype(f32)
    ratio = degree * (degree + 1.0) * (1.0 / (TRUNC * (TRUNC - 1.0)))
    response = 1.0 / (1.0 + damping * ratio * ratio)
    response = jnp.concatenate([response, response], axis=0)

    for i in range(N_LAT):
        rs[i] = four_ref[i].astype(f32)
    flat = rs.reshape(N_LAT * PAD, 128)
    turned = []
    for q in range(4):
        block = jnp.concatenate(
            [flat[pl.ds(4 * q + i, N_LAT, stride=PAD), :] for i in range(4)], axis=0
        )
        turned.append(block.T)

    def rows_of(kj):
        piece = turned[kj // 4]
        low = 32 * (kj % 4)
        return jnp.concatenate(
            [piece[PAD * a : PAD * (a + 1), low : low + 32] for a in range(ROWS)], axis=1
        )

    made = [None] * 16
    for j in range(WAVES):
        field = jnp.concatenate([rows_of(j), rows_of(8 + j)], axis=0).astype(bf16)
        left = table[pl.ds(j, TRUNC, stride=WAVES), :]
        right = table[pl.ds(HALF + j, TRUNC, stride=WAVES), :]
        high, low = split(jnp.concatenate([left, right], axis=1))
        coeffs = (mm_nt(field, high) + mm_nt(field, low)) * response
        for k in range(2):
            for f in range(4):
                at = PAD * k + 3 * f
                spec_ref[j, k, f] = coeffs[at : at + 3, :]
        ch, cl = split(coeffs)
        grid = mm(ch, high) + mm(cl, high) + mm(ch, low)
        made[j] = grid[:PAD]
        made[8 + j] = grid[PAD:]
    flat_out = so.reshape(N_LAT * PAD, 128)
    for q in range(4):
        block = jnp.concatenate(
            [
                jnp.concatenate(
                    [made[4 * q + i][:, 32 * a : 32 * (a + 1)] for i in range(4)], axis=1
                )
                for a in range(ROWS)
            ],
            axis=0,
        )
        back = block.T
        for i in range(4):
            flat_out[pl.ds(4 * q + i, N_LAT, stride=PAD), :] = back[32 * i : 32 * (i + 1)]


def inverse(syn_ref, high_ref, low_ref, order_ref, scale_ref, in_ref, turn, lev):
    onehot = wave_onehot(order_ref)
    factor = jnp.where(iota((TRUNC, 128), 0) == 0, 1.0, 2.0)
    parts = []
    for k in range(2):
        part_high, part_low = split(syn_ref[:, 8 * k : 8 * (k + 1), :].reshape(TRUNC, 128))
        parts.append(((mm(onehot, part_high) + mm(onehot, part_low)) * factor).T)
    mh, ml = split(jnp.concatenate(parts, axis=1))
    rows = mm_nt(mh, high_ref[...]) + mm_nt(ml, high_ref[...]) + mm_nt(mh, low_ref[...])
    pair = iota((PAD, NLON), 0)
    scale = jnp.zeros((PAD, NLON), f32)
    for i in range(USED):
        scale = jnp.where(pair == i, scale_ref[i // 3, lev * 3 + i % 3], scale)
    for a in range(ROWS):
        piece = rows[PAD * a : PAD * (a + 1), :]
        in_ref[a] = (piece * scale).astype(bf16)
        for c in range(NLON // 128):
            turn[pl.ds(96 * c + a, USED, stride=ROWS), :] = piece[:USED, 128 * c : 128 * (c + 1)]


def prepare(win_ref, bin_ref, wmid_ref, bmid_ref, wout_ref, win_s, wout_s, woutT_s, wmidT_s, bin_s, bmid_s):
    win_s[...] = mm(win_ref[...], feature_onehot((96, 128), 0)).astype(bf16)
    wout = mm(feature_onehot((128, 96), 1), wout_ref[...])
    wout_s[...] = wout.astype(bf16)
    woutT_s[...] = wout.T.astype(bf16)
    wmidT_s[...] = wmid_ref[...].astype(f32).T.astype(bf16)
    bin_s[...] = jnp.broadcast_to(bin_ref[...], (128, 512)).T
    bmid_s[...] = jnp.broadcast_to(bmid_ref[...], (128, 512)).T


def activation(value):
    z = 0.5 + 0.5 * jnp.tanh(0.5 * value)
    return value * z, z * (1.0 + value * (1.0 - z))


def columns(c):
    return pl.ds(pl.multiple_of(c * 256, 256), 256)


def greet(axes):
    barrier = pltpu.get_barrier_semaphore()
    for axis, size in axes:
        me = lax.axis_index(axis)

        def signal(d, _):
            peer = lax.rem(me + d, size)
            pl.semaphore_signal(barrier, inc=1, device_id={axis: peer}, device_id_type=MESH)
            return 0

        lax.fori_loop(1, size, signal, 0)
    return lambda: pl.semaphore_wait(barrier, sum(size - 1 for _, size in axes))


def scatter(axis, size, source, landing, send, recv):
    me = lax.axis_index(axis)

    def copy(d):
        peer = lax.rem(me + d, size)
        return pltpu.make_async_remote_copy(
            src_ref=source(peer), dst_ref=landing.at[me], send_sem=send.at[d],
            recv_sem=recv.at[d], device_id={axis: peer}, device_id_type=MESH,
        )

    def start(d, _):
        copy(d).start()
        return 0

    def wait(d, _):
        copy(d).wait()
        return 0

    lax.fori_loop(1, size, start, 0)
    return lambda: lax.fori_loop(1, size, wait, 0)


def total_of(ref):
    def body(i, acc):
        return acc + ref[i].astype(f32)

    return lax.fori_loop(1, ref.shape[0], body, ref[0].astype(f32))


def step_kernel(
    x_ref, ct_ref, high_ref, low_ref, order_ref, lat_ref, diag_ref, deg_ref, damp_ref, scale_ref,
    win_ref, bin_ref, wmid_ref, bmid_ref, wout_ref,
    spec_ref, state_ref, tot0, tot1, tot2, tot3,
    rows, xs, fs, up_send, up_in, four_send, four_in, table, so, syn_in, turn, in_send, in_in,
    win_s, wout_s, woutT_s, wmidT_s, bin_s, bmid_s, in_s, up_s, bm_s, h_in_s, slope_s, h_mid_s,
    d_mid_s, d_in_s, gbm, tend_s, tend_send, tend_in,
    send0, send1, send2, send3, part0, part1, part2, part3,
    piece0, piece1, piece2, piece3, pieces0, pieces1, pieces2, pieces3, done0, done1, done2, done3,
    *semaphores,
):
    lat, lev = lax.axis_index("lat"), lax.axis_index("lev")
    pairs = iter([semaphores[i : i + 2] for i in range(0, len(semaphores), 2)])
    met = greet((("lat", N_LAT), ("lev", N_LEV)))

    def to_lat(source, landing):
        return scatter("lat", N_LAT, source, landing, *next(pairs))

    def to_lev(source, landing):
        return scatter("lev", N_LEV, source, landing, *next(pairs))

    xs[...] = jnp.zeros_like(xs)
    take_rows(rows, ct_ref, xs)
    for a in range(ROWS):
        up_send[a] = xs[PAD * a : PAD * (a + 1), :].astype(bf16)
    forward(x_ref, high_ref, low_ref, order_ref, lat_ref, rows, xs, fs, four_send, lat)
    met()
    wait_four = to_lat(lambda p: four_send.at[p], four_in)
    wait_up = to_lev(lambda p: up_send.at[p], up_in)
    four_in[lat] = four_send[lat]
    up_in[lev] = up_send[lev]
    legendre_table(order_ref, lat_ref, diag_ref, deg_ref, table, lat)
    wait_four()
    analysis(four_in, damp_ref, spec_ref, table, fs, so)
    wait_syn = to_lat(lambda p: so.at[p], syn_in)
    syn_in[lat] = so[lat]
    prepare(
        win_ref, bin_ref, wmid_ref, bmid_ref, wout_ref, win_s, wout_s, woutT_s, wmidT_s, bin_s, bmid_s
    )
    wait_syn()
    inverse(syn_in, high_ref, low_ref, order_ref, scale_ref, in_send, turn, lev)
    wait_in = to_lev(lambda p: in_send.at[p], in_in)
    in_in[lev] = in_send[lev]
    wait_up()
    up_s[...] = up_in[...].reshape(128, NLON)

    def back_chunk(c, _):
        bm_s[:, columns(c)] = mm(woutT_s[...], up_s[:, columns(c)])
        return 0

    lax.fori_loop(0, 3, back_chunk, 0)
    gbm[...] = jnp.zeros_like(gbm)
    wait_in()
    inputs = in_in[...].reshape(128, NLON)
    in_s[...] = jnp.where(iota((128, NLON), 0) == USED, 1.0, inputs.astype(f32)).astype(bf16)

    def chunk(c, _):
        cols = columns(c)
        b_in = jnp.concatenate([bin_s[...], bin_s[...]], axis=1)
        h_in, slope_in = activation(mm(win_s[...], in_s[:, cols]) + b_in)
        h_in = h_in.astype(bf16)
        h_in_s[:, cols] = h_in
        slope_s[:, cols] = slope_in
        b_mid = jnp.concatenate([bmid_s[...], bmid_s[...]], axis=1)
        h_mid, slope_mid = activation(mm(wmid_ref[...], h_in) + b_mid)
        h_mid = h_mid.astype(bf16)
        h_mid_s[:, cols] = h_mid
        tend_s[:, cols] = mm(wout_s[...], h_mid).astype(bf16)
        d_mid = (bm_s[:, cols] * slope_mid).astype(bf16)
        d_mid_s[:, cols] = d_mid
        wide = d_mid.astype(f32)
        gbm[...] += wide[:, :128] + wide[:, 128:]
        return 0

    lax.fori_loop(0, 3, chunk, 0)
    tend_send[...] = tend_s[...].reshape(N_LEV, PAD, NLON)
    norm = 1.0 / math.sqrt(256 * NLON)

    def packed(value):
        return (value * norm).astype(bf16).reshape(N_LAT, 16, value.shape[1])

    bias = jnp.sum(gbm[...], axis=1, keepdims=True)
    gout = mm_nt(h_mid_s[...], up_s[...])
    send0[...] = packed(jnp.where(iota((512, 128), 1) == USED, bias, gout))
    wait_part0 = to_lat(lambda p: send0.at[p], part0)
    wait_tend = to_lev(lambda p: tend_send.at[p], tend_in)
    part0[lat] = send0[lat]
    tend_in[lev] = tend_send[lev]
    send1[...] = packed(mm_nt(d_mid_s[...], h_in_s[0:256, :]))
    wait_part1 = to_lat(lambda p: send1.at[p], part1)
    part1[lat] = send1[lat]
    send2[...] = packed(mm_nt(d_mid_s[...], h_in_s[256:512, :]))
    wait_part2 = to_lat(lambda p: send2.at[p], part2)
    part2[lat] = send2[lat]

    def delta_chunk(c, _):
        cols = columns(c)
        d_in_s[:, cols] = (mm(wmidT_s[...], d_mid_s[:, cols]) * slope_s[:, cols]).astype(bf16)
        return 0

    lax.fori_loop(0, 3, delta_chunk, 0)
    send3[...] = packed(mm_nt(d_in_s[...], in_s[...]))
    wait_part3 = to_lat(lambda p: send3.at[p], part3)
    part3[lat] = send3[lat]

    waits = []
    for wait, part, piece, pieces in (
        (wait_part0, part0, piece0, pieces0), (wait_part1, part1, piece1, pieces1),
        (wait_part2, part2, piece2, pieces2), (wait_part3, part3, piece3, pieces3),
    ):
        wait()
        piece[...] = total_of(part).astype(bf16)
        waits.append(to_lev(lambda p, piece=piece: piece, pieces))
        pieces[lev] = piece[...]
    finals = []
    for wait, pieces, done, tot in zip(
        waits, (pieces0, pieces1, pieces2, pieces3), (done0, done1, done2, done3),
        (tot0, tot1, tot2, tot3),
    ):
        wait()
        done[...] = total_of(pieces).astype(bf16)
        finals.append(to_lat(lambda p, done=done: done, tot))
        tot[lat] = done[...]
    wait_tend()
    for a in range(ROWS):
        piece = tend_in[a].astype(f32)
        for c in range(NLON // 128):
            at = pl.ds(96 * c + a, USED, stride=ROWS)
            turn[at, :] = turn[at, :] + piece[:USED, 128 * c : 128 * (c + 1)]
    for c in range(NLON // 128):
        state_ref[:, 128 * c : 128 * (c + 1)] = turn[96 * c : 96 * (c + 1), :]
    for wait in finals:
        wait()


def finish_kernel(tot0, tot1, tot2, tot3, gin_ref, gbin_ref, gmid_ref, gbmid_ref, gout_ref):
    last, first = tot0[...].reshape(512, 128), tot3[...].reshape(512, 128)
    gin_ref[...] = mm(first, feature_onehot((128, 96), 1))
    gout_ref[...] = mm_nt(feature_onehot((96, 128), 0), last)
    gmid_ref[:, :256] = tot1[...].reshape(512, 256).astype(f32)
    gmid_ref[:, 256:] = tot2[...].reshape(512, 256).astype(f32)
    pick = (iota((8, 128), 1) == USED).astype(f32).astype(bf16)
    gbin_ref[...] = mm_nt(pick, first)[:1]
    gbmid_ref[...] = mm_nt(pick, last)[:1]


def like(shape, dtype):
    return jax.ShapeDtypeStruct(shape, dtype)


def sems(count):
    return [pltpu.SemaphoreType.DMA((count,)), pltpu.SemaphoreType.DMA((count,))]


def on_device(
    prognostic, cotangent, damping, in_scale, w_in, b_in, w_mid, b_mid, w_out, wave_order, lat_order
):
    high, low = dft_tables()
    order = wave_order.reshape(1, TRUNC)
    lats = lat_order.reshape(1, 256)
    count = ROWS * USED
    waves16 = pltpu.VMEM((N_LAT, PAD, 128), bf16)
    waves32 = pltpu.VMEM((N_LAT, PAD, 128), f32)
    blocks = pltpu.VMEM((N_LEV, PAD, NLON), bf16)
    wide16 = pltpu.VMEM((512, NLON), bf16)
    wide32 = pltpu.VMEM((512, NLON), f32)
    skinny = pltpu.VMEM((128, NLON), bf16)
    widths = (128, 256, 256, 128)

    def per_piece(*leading):
        return [pltpu.VMEM((*leading, 16, width), bf16) for width in widths]

    scratch = [
        pltpu.VMEM((576, 128), f32), pltpu.VMEM((128, NLON), f32), waves32, blocks, blocks,
        waves16, waves16, pltpu.VMEM((2 * HALF, 128), f32), waves32, waves32,
        pltpu.VMEM((576, 128), f32), blocks, blocks,
        pltpu.VMEM((512, 128), bf16), pltpu.VMEM((128, 512), bf16), pltpu.VMEM((512, 128), bf16),
        pltpu.VMEM((512, 512), bf16), pltpu.VMEM((512, 128), f32), pltpu.VMEM((512, 128), f32),
        skinny, skinny, wide32, wide16, wide32, wide16, wide16, wide16,
        pltpu.VMEM((512, 128), f32), skinny, blocks, blocks,
        *per_piece(N_LAT), *per_piece(N_LAT), *per_piece(), *per_piece(N_LEV), *per_piece(),
    ]
    lat_sems, lev_sems = sems(N_LAT), sems(N_LEV)
    scratch += lat_sems + lev_sems + lat_sems + lev_sems
    scratch += lat_sems + lev_sems + lat_sems * 3
    scratch += lev_sems * 4 + lat_sems * 4
    spectral, state, *totals = pl.pallas_call(
        step_kernel,
        out_shape=[
            like((WAVES, 2, 4, 3, TRUNC), f32), like((count, NLON), f32),
            *[like((N_LAT, 16, width), bf16) for width in widths],
        ],
        in_specs=[VMEM] * 7 + [SMEM] * 3 + [VMEM] * 5,
        out_specs=[VMEM] * 6,
        scratch_shapes=scratch,
        compiler_params=pltpu.CompilerParams(collective_id=0, has_side_effects=True),
        name="step",
    )(
        prognostic.reshape(count, NLON), cotangent.reshape(count, NLON), high, low, order, lats,
        diagonal_table(), degree_table(), damping, in_scale,
        w_in, b_in.reshape(1, 512), w_mid, b_mid.reshape(1, 512), w_out,
    )
    gin, gbin, gmid, gbmid, gout = pl.pallas_call(
        finish_kernel,
        out_shape=[
            like((512, 96), f32), like((1, 512), f32), like((512, 512), f32), like((1, 512), f32),
            like((96, 512), f32),
        ],
        in_specs=[VMEM] * 4,
        out_specs=[VMEM] * 5,
        name="finish",
    )(*totals)
    return (
        state.reshape(prognostic.shape), spectral, gin, gbin.reshape(512), gmid, gbmid.reshape(512), gout,
    )


def solution(mesh):
    return jax.shard_map(
        on_device,
        mesh=mesh,
        in_specs=(
            P(None, "lev", "lat", None),
            P(None, "lev", "lat", None),
            P(None, "lev"),
            P(),
            P(),
            P(),
            P(),
            P(),
            P(),
            P(),
            P(),
        ),
        out_specs=(
            P(None, "lev", "lat", None),
            P("lat", None, None, "lev", None),
            P(),
            P(),
            P(),
            P(),
            P(),
        ),
        check_vma=False,
    )
```

time: 116 us -> 84.9 us (0.73)
  Pallas kernels: 111 us -> 78.2 us
  local copies, waits for them, and re-layouts: 4.14 us -> 5.84 us
    pallas_call x9 -> x2, Pallas kernels: 111 us -> 78.2 us  [the longest x1 75.7 us: on_device(): pl.pallas_call(step_kernel, out_shape=[like((WAVES, 2, 4, 3, TRUNC), f32)...]
    unnamed x5 -> x6, local copies, waits for them, and re-layouts: 4.14 us -> 5.84 us
where the time goes in v2:
time: 84.9 us; the launch traced here: 84.6 us
  Pallas kernels  78.2 us (92%)
  local copies, waits for them, and re-layouts  5.84 us (7%)
    pallas_call x1, Pallas kernels, on_device(): pl.pallas_call(step_kernel, out_shape=[like((WAVES, 2, 4, 3, TRUNC), f32)...  75.7 us
    unnamed x6, local copies, waits for them, and re-layouts  5.84 us
    pallas_call x1, Pallas kernels, on_device(): pl.pallas_call(finish_kernel, out_shape=[like((512, 96), f32), like((1, 5...  2.5 us

profile of v2, /device:TPU:1, one launch (start us, length us, event | category | flops | bytes accessed | tf_op | source)
XLA Modules:
  0.0 84.6 jit_solution(15901516237959615679)
XLA Ops:
  0.6 1.7 %copy.22.win_ref = bf16[512,96]{1,0:T(8,128)(2,1)} copy(bf16[512,96]{0,1:T(8,128)(2,1)} %param.19) | data formatting | bytes 196608 | tf_op args[4]
  2.3 75.7 %step.1 = (f32[8,2,4,3,256]{4,3,2,1,0:T(4,128)}, f32[96,768]{1,0:T(8,128)}, bf16[32,16,128]{2,1,0:T(8,128)(2,1)}, bf16[32,16,256]{2,1,0:T(8,128)(2,1)}, bf16[32,...) custom-call(f32[96,768]{1,0:T(8,128)} %bitcast.9, bf16[96,768]{1,0:T(8,128)(2,1)} %bitcast.11, ...), custom_call_target="tpu_custom_call" | custom-call | tf_op jit(solution)/shard_map/step/pallas_call | solution.py:482
  78.0 1.7 %copy.23 = f32[8,2,4,3,256]{4,2,3,1,0:T(4,128)} copy(f32[8,2,4,3,256]{4,3,2,1,0:T(4,128)} %get-tuple-element.30) | data formatting | bytes 393216
  79.6 2.5 %finish.1 = (f32[512,96]{1,0:T(8,128)}, f32[1,512]{1,0:T(1,128)}, f32[512,512]{1,0:T(8,128)}, f32[1,512]{1,0:T(1,128)}, f32[96,512]{1,0:T(8,128)}) custom-call(bf16[32,16,128]{2,1,0:T(8,128)(2,1)} %get-tuple-element.20.tot0, bf16[32,16,256]{2,1,0:T(8,128)(2,1)} %get-tuple-element.21.tot1, bf16[32,16,256]{2,1,0:T(8,128)(2,1)} %get-tuple-element.22.tot2, ...), custom_call_target="tpu_custom_call" | custom-call | tf_op jit(solution)/shard_map/finish/pallas_call | solution.py:498
  82.1 0.0 copy-start
  82.1 1.8 %copy.24 = f32[512,96]{0,1:T(8,128)} copy(f32[512,96]{1,0:T(8,128)} %get-tuple-element.31) | data formatting | bytes 393216
  83.9 0.0 copy-done
  83.9 0.7 copy.26
Async XLA Ops:
  82.1 1.8 %copy-start = (f32[96,768]{1,0:T(8,128)S(1)}, f32[96,768]{1,0:T(8,128)}, u32[]{:S(2)}) copy-start(f32[96,768]{1,0:T(8,128)} %get-tuple-element.18) | copy-start | bytes 884740

commit v3 on v2

--- a/solution.py
+++ b/solution.py
@@ -73,10 +73,7 @@
 
 def feature_of(column):
     lev, pair = column // PAD, column % PAD
-    field = (
-        (pair >= 3).astype(jnp.int32) + (pair >= 6).astype(jnp.int32) + (pair >= 9).astype(jnp.int32)
-    )
-    feature = field * 24 + lev * 3 + pair - field * 3
+    feature = (pair % 4) * 24 + lev * 3 + pair // 4
     return jnp.where(pair < USED, feature, -1)
 
 
@@ -85,9 +82,16 @@
     return (iota(shape, feature_axis) == column).astype(f32).astype(bf16)
 
 
+def stored(i):
+    return (i % 4) * 3 + i // 4
+
+
 def take_rows(rows, source, target):
     for c in range(NLON // 128):
-        rows[96 * c : 96 * (c + 1), :] = source[:, 128 * c : 128 * (c + 1)].astype(f32)
+        value = source[:, 128 * c : 128 * (c + 1)].astype(f32)
+        for i in range(USED):
+            at = 96 * c + ROWS * i
+            rows[at : at + ROWS, :] = value[ROWS * stored(i) : ROWS * (stored(i) + 1), :]
         for a in range(ROWS):
             picked = rows[pl.ds(96 * c + a, USED, stride=ROWS), :]
             target[PAD * a : PAD * a + USED, 128 * c : 128 * (c + 1)] = picked
@@ -157,7 +161,7 @@
     pair = iota((PAD, 256), 0)
     damping = jnp.zeros((PAD, 256), f32)
     for i in range(USED):
-        damping = jnp.where(pair == i, damp_ref[i // 3, i % 3], damping)
+        damping = jnp.where(pair == i, damp_ref[i % 4, i // 4], damping)
     degree = iota((PAD, 256), 1).astype(f32)
     ratio = degree * (degree + 1.0) * (1.0 / (TRUNC * (TRUNC - 1.0)))
     response = 1.0 / (1.0 + damping * ratio * ratio)
@@ -188,9 +192,9 @@
         high, low = split(jnp.concatenate([left, right], axis=1))
         coeffs = (mm_nt(field, high) + mm_nt(field, low)) * response
         for k in range(2):
-            for f in range(4):
-                at = PAD * k + 3 * f
-                spec_ref[j, k, f] = coeffs[at : at + 3, :]
+            for e in range(3):
+                at = PAD * k + 4 * e
+                spec_ref[j, k, e] = coeffs[at : at + 4, :]
         ch, cl = split(coeffs)
         grid = mm(ch, high) + mm(cl, high) + mm(ch, low)
         made[j] = grid[:PAD]
@@ -211,28 +215,29 @@
             flat_out[pl.ds(4 * q + i, N_LAT, stride=PAD), :] = back[32 * i : 32 * (i + 1)]
 
 
-def inverse(syn_ref, high_ref, low_ref, order_ref, scale_ref, in_ref, turn, lev):
+def mode_rows(syn_ref, order_ref, mh_s, ml_s):
     onehot = wave_onehot(order_ref)
     factor = jnp.where(iota((TRUNC, 128), 0) == 0, 1.0, 2.0)
-    parts = []
     for k in range(2):
         part_high, part_low = split(syn_ref[:, 8 * k : 8 * (k + 1), :].reshape(TRUNC, 128))
-        parts.append(((mm(onehot, part_high) + mm(onehot, part_low)) * factor).T)
-    mh, ml = split(jnp.concatenate(parts, axis=1))
-    rows = mm_nt(mh, high_ref[...]) + mm_nt(ml, high_ref[...]) + mm_nt(mh, low_ref[...])
-    pair = iota((PAD, NLON), 0)
-    scale = jnp.zeros((PAD, NLON), f32)
-    for i in range(USED):
-        scale = jnp.where(pair == i, scale_ref[i // 3, lev * 3 + i % 3], scale)
+        part = ((mm(onehot, part_high) + mm(onehot, part_low)) * factor).T
+        mh_s[:, 256 * k : 256 * (k + 1)], ml_s[:, 256 * k : 256 * (k + 1)] = split(part)
+
+
+def inverse(mh_s, ml_s, high_ref, low_ref, scale, in_ref, turn, chunk):
+    points = slice(256 * chunk, 256 * (chunk + 1))
+    high = high_ref[points, :]
+    rows = mm_nt(mh_s[...], high) + mm_nt(ml_s[...], high) + mm_nt(mh_s[...], low_ref[points, :])
     for a in range(ROWS):
         piece = rows[PAD * a : PAD * (a + 1), :]
         in_ref[a] = (piece * scale).astype(bf16)
-        for c in range(NLON // 128):
-            turn[pl.ds(96 * c + a, USED, stride=ROWS), :] = piece[:USED, 128 * c : 128 * (c + 1)]
+        for half in range(2):
+            at = pl.ds(96 * (2 * chunk + half) + a, USED, stride=ROWS)
+            turn[at, :] = piece[:USED, 128 * half : 128 * (half + 1)]
 
 
 def prepare(win_ref, bin_ref, wmid_ref, bmid_ref, wout_ref, win_s, wout_s, woutT_s, wmidT_s, bin_s, bmid_s):
-    win_s[...] = mm(win_ref[...], feature_onehot((96, 128), 0)).astype(bf16)
+    win_s[...] = mm(feature_onehot((128, 96), 1), win_ref[...]).T.astype(bf16)
     wout = mm(feature_onehot((128, 96), 1), wout_ref[...])
     wout_s[...] = wout.astype(bf16)
     woutT_s[...] = wout.T.astype(bf16)
@@ -264,13 +269,13 @@
     return lambda: pl.semaphore_wait(barrier, sum(size - 1 for _, size in axes))
 
 
-def scatter(axis, size, source, landing, send, recv):
+def scatter(axis, size, source, landing, send, recv, stride=1):
     me = lax.axis_index(axis)
 
     def copy(d):
-        peer = lax.rem(me + d, size)
+        peer = lax.rem(me + d * stride, size)
         return pltpu.make_async_remote_copy(
-            src_ref=source(peer), dst_ref=landing.at[me], send_sem=send.at[d],
+            src_ref=source(peer), dst_ref=landing, send_sem=send.at[d],
             recv_sem=recv.at[d], device_id={axis: peer}, device_id_type=MESH,
         )
 
@@ -282,8 +287,8 @@
         copy(d).wait()
         return 0
 
-    lax.fori_loop(1, size, start, 0)
-    return lambda: lax.fori_loop(1, size, wait, 0)
+    lax.fori_loop(1, size // stride, start, 0)
+    return lambda: lax.fori_loop(1, size // stride, wait, 0)
 
 
 def total_of(ref):
@@ -296,23 +301,34 @@
 def step_kernel(
     x_ref, ct_ref, high_ref, low_ref, order_ref, lat_ref, diag_ref, deg_ref, damp_ref, scale_ref,
     win_ref, bin_ref, wmid_ref, bmid_ref, wout_ref,
-    spec_ref, state_ref, tot0, tot1, tot2, tot3,
-    rows, xs, fs, up_send, up_in, four_send, four_in, table, so, syn_in, turn, in_send, in_in,
+    spec_ref, state_ref, tot0, tot1, tot2,
+    rows, xs, fs, up_send, up_in, four_send, four_in, table, so, syn_in, turn, mh_s, ml_s,
+    in_send0, in_send1, in_send2, in_in0, in_in1, in_in2,
     win_s, wout_s, woutT_s, wmidT_s, bin_s, bmid_s, in_s, up_s, bm_s, h_in_s, slope_s, h_mid_s,
     d_mid_s, d_in_s, gbm, tend_s, tend_send, tend_in,
-    send0, send1, send2, send3, part0, part1, part2, part3,
-    piece0, piece1, piece2, piece3, pieces0, pieces1, pieces2, pieces3, done0, done1, done2, done3,
+    send0, send1, send2, pair0, pair1, pair2, sum0, sum1, sum2, part0, part1, part2,
+    piece0, piece1, piece2, pieces0, pieces1, pieces2, done0, done1, done2,
     *semaphores,
 ):
     lat, lev = lax.axis_index("lat"), lax.axis_index("lev")
+    core, column = lax.rem(lev, 2), lev // 2
     pairs = iter([semaphores[i : i + 2] for i in range(0, len(semaphores), 2)])
     met = greet((("lat", N_LAT), ("lev", N_LEV)))
 
     def to_lat(source, landing):
         return scatter("lat", N_LAT, source, landing, *next(pairs))
 
-    def to_lev(source, landing):
-        return scatter("lev", N_LEV, source, landing, *next(pairs))
+    def to_lev(source, landing, stride=1):
+        return scatter("lev", N_LEV, source, landing, *next(pairs), stride=stride)
+
+    def to_partner(source, landing):
+        send, recv = next(pairs)
+        copy = pltpu.make_async_remote_copy(
+            src_ref=source, dst_ref=landing, send_sem=send.at[0], recv_sem=recv.at[0],
+            device_id={"lev": lev + 1 - 2 * core}, device_id_type=MESH,
+        )
+        copy.start()
+        return copy.wait
 
     xs[...] = jnp.zeros_like(xs)
     take_rows(rows, ct_ref, xs)
@@ -320,22 +336,32 @@
         up_send[a] = xs[PAD * a : PAD * (a + 1), :].astype(bf16)
     forward(x_ref, high_ref, low_ref, order_ref, lat_ref, rows, xs, fs, four_send, lat)
     met()
-    wait_four = to_lat(lambda p: four_send.at[p], four_in)
-    wait_up = to_lev(lambda p: up_send.at[p], up_in)
+    wait_four = to_lat(lambda p: four_send.at[p], four_in.at[lat])
+    wait_up = to_lev(lambda p: up_send.at[p], up_in.at[lev])
     four_in[lat] = four_send[lat]
     up_in[lev] = up_send[lev]
     legendre_table(order_ref, lat_ref, diag_ref, deg_ref, table, lat)
     wait_four()
     analysis(four_in, damp_ref, spec_ref, table, fs, so)
-    wait_syn = to_lat(lambda p: so.at[p], syn_in)
+    wait_syn = to_lat(lambda p: so.at[p], syn_in.at[lat])
     syn_in[lat] = so[lat]
     prepare(
         win_ref, bin_ref, wmid_ref, bmid_ref, wout_ref, win_s, wout_s, woutT_s, wmidT_s, bin_s, bmid_s
     )
+    pair = iota((PAD, 256), 0)
+    scale = jnp.zeros((PAD, 256), f32)
+    for i in range(USED):
+        scale = jnp.where(pair == i, scale_ref[i % 4, lev * 3 + i // 4], scale)
+    gbm[...] = jnp.zeros_like(gbm)
     wait_syn()
-    inverse(syn_in, high_ref, low_ref, order_ref, scale_ref, in_send, turn, lev)
-    wait_in = to_lev(lambda p: in_send.at[p], in_in)
-    in_in[lev] = in_send[lev]
+    mode_rows(syn_in, order_ref, mh_s, ml_s)
+    wait_ins = []
+    for c, (in_send, in_in) in enumerate(
+        ((in_send0, in_in0), (in_send1, in_in1), (in_send2, in_in2))
+    ):
+        inverse(mh_s, ml_s, high_ref, low_ref, scale, in_send, turn, c)
+        wait_ins.append(to_lev(lambda p, in_send=in_send: in_send.at[p], in_in.at[lev]))
+        in_in[lev] = in_send[lev]
     wait_up()
     up_s[...] = up_in[...].reshape(128, NLON)
 
@@ -344,15 +370,15 @@
         return 0
 
     lax.fori_loop(0, 3, back_chunk, 0)
-    gbm[...] = jnp.zeros_like(gbm)
-    wait_in()
-    inputs = in_in[...].reshape(128, NLON)
-    in_s[...] = jnp.where(iota((128, NLON), 0) == USED, 1.0, inputs.astype(f32)).astype(bf16)
-
-    def chunk(c, _):
-        cols = columns(c)
+    ones = iota((128, 256), 0) == USED
+    for c, in_in in enumerate((in_in0, in_in1, in_in2)):
+        cols = slice(256 * c, 256 * (c + 1))
+        wait_ins[c]()
+        inputs = in_in[...].reshape(128, 256)
+        inputs = jnp.where(ones, 1.0, inputs.astype(f32)).astype(bf16)
+        in_s[:, cols] = inputs
         b_in = jnp.concatenate([bin_s[...], bin_s[...]], axis=1)
-        h_in, slope_in = activation(mm(win_s[...], in_s[:, cols]) + b_in)
+        h_in, slope_in = activation(mm(win_s[...], inputs) + b_in)
         h_in = h_in.astype(bf16)
         h_in_s[:, cols] = h_in
         slope_s[:, cols] = slope_in
@@ -365,28 +391,34 @@
         d_mid_s[:, cols] = d_mid
         wide = d_mid.astype(f32)
         gbm[...] += wide[:, :128] + wide[:, 128:]
-        return 0
-
-    lax.fori_loop(0, 3, chunk, 0)
     tend_send[...] = tend_s[...].reshape(N_LEV, PAD, NLON)
     norm = 1.0 / math.sqrt(256 * NLON)
 
     def packed(value):
-        return (value * norm).astype(bf16).reshape(N_LAT, 16, value.shape[1])
-
-    bias = jnp.sum(gbm[...], axis=1, keepdims=True)
-    gout = mm_nt(h_mid_s[...], up_s[...])
-    send0[...] = packed(jnp.where(iota((512, 128), 1) == USED, bias, gout))
-    wait_part0 = to_lat(lambda p: send0.at[p], part0)
-    wait_tend = to_lev(lambda p: tend_send.at[p], tend_in)
-    part0[lat] = send0[lat]
+        return (value * norm).astype(bf16).reshape(N_LAT, 16, 128)
+
+    def offer(send, pair):
+        return to_partner(send.at[1 - core], pair)
+
+    def reduce_scatter(wait, send, pair, total, part):
+        wait()
+        total[...] = (send[core].astype(f32) + pair[...].astype(f32)).astype(bf16)
+        part[lat] = total[lat]
+        return to_lat(lambda p: total.at[p], part.at[lat])
+
+    def mid_unit(send, at):
+        chosen = jnp.concatenate([h_in_s[at : at + 128, :], h_in_s[at + 256 : at + 384, :]], axis=0)
+        value = mm_nt(d_mid_s[...], chosen)
+        send[0] = packed(value[:, :128])
+        send[1] = packed(value[:, 128:])
+
+    mid_unit(send0, 0)
+    offered0 = offer(send0, pair0)
+    mid_unit(send1, 128)
+    offered1 = offer(send1, pair1)
+    wait_tend = to_lev(lambda p: tend_send.at[p], tend_in.at[lev])
     tend_in[lev] = tend_send[lev]
-    send1[...] = packed(mm_nt(d_mid_s[...], h_in_s[0:256, :]))
-    wait_part1 = to_lat(lambda p: send1.at[p], part1)
-    part1[lat] = send1[lat]
-    send2[...] = packed(mm_nt(d_mid_s[...], h_in_s[256:512, :]))
-    wait_part2 = to_lat(lambda p: send2.at[p], part2)
-    part2[lat] = send2[lat]
+    wait_part0 = reduce_scatter(offered0, send0, pair0, sum0, part0)
 
     def delta_chunk(c, _):
         cols = columns(c)
@@ -394,28 +426,31 @@
         return 0
 
     lax.fori_loop(0, 3, delta_chunk, 0)
-    send3[...] = packed(mm_nt(d_in_s[...], in_s[...]))
-    wait_part3 = to_lat(lambda p: send3.at[p], part3)
-    part3[lat] = send3[lat]
+    bias = jnp.sum(gbm[...], axis=1, keepdims=True)
+    gout = mm_nt(h_mid_s[...], up_s[...])
+    send2[0] = packed(jnp.where(iota((512, 128), 1) == USED, bias, gout))
+    send2[1] = packed(mm_nt(d_in_s[...], in_s[...]))
+    offered2 = offer(send2, pair2)
+    wait_part1 = reduce_scatter(offered1, send1, pair1, sum1, part1)
+    wait_part2 = reduce_scatter(offered2, send2, pair2, sum2, part2)
 
     waits = []
     for wait, part, piece, pieces in (
         (wait_part0, part0, piece0, pieces0), (wait_part1, part1, piece1, pieces1),
-        (wait_part2, part2, piece2, pieces2), (wait_part3, part3, piece3, pieces3),
+        (wait_part2, part2, piece2, pieces2),
     ):
         wait()
-        piece[...] = total_of(part).astype(bf16)
-        waits.append(to_lev(lambda p, piece=piece: piece, pieces))
-        pieces[lev] = piece[...]
-    finals = []
+        piece[...] = total_of(part)
+        waits.append(to_lev(lambda p, piece=piece: piece, pieces.at[column], stride=2))
+        pieces[column] = piece[...]
+    gathers = []
     for wait, pieces, done, tot in zip(
-        waits, (pieces0, pieces1, pieces2, pieces3), (done0, done1, done2, done3),
-        (tot0, tot1, tot2, tot3),
+        waits, (pieces0, pieces1, pieces2), (done0, done1, done2), (tot0, tot1, tot2)
     ):
         wait()
         done[...] = total_of(pieces).astype(bf16)
-        finals.append(to_lat(lambda p, done=done: done, tot))
-        tot[lat] = done[...]
+        gathers.append(to_lat(lambda p, done=done: done, tot.at[core, lat]))
+        tot[core, lat] = done[...]
     wait_tend()
     for a in range(ROWS):
         piece = tend_in[a].astype(f32)
@@ -423,17 +458,32 @@
             at = pl.ds(96 * c + a, USED, stride=ROWS)
             turn[at, :] = turn[at, :] + piece[:USED, 128 * c : 128 * (c + 1)]
     for c in range(NLON // 128):
-        state_ref[:, 128 * c : 128 * (c + 1)] = turn[96 * c : 96 * (c + 1), :]
-    for wait in finals:
+        for i in range(USED):
+            at = 96 * c + ROWS * i
+            state_ref[ROWS * stored(i) : ROWS * (stored(i) + 1), 128 * c : 128 * (c + 1)] = turn[
+                at : at + ROWS, :
+            ]
+    handed = []
+    for wait, tot in zip(gathers, (tot0, tot1, tot2)):
         wait()
-
-
-def finish_kernel(tot0, tot1, tot2, tot3, gin_ref, gbin_ref, gmid_ref, gbmid_ref, gout_ref):
-    last, first = tot0[...].reshape(512, 128), tot3[...].reshape(512, 128)
-    gin_ref[...] = mm(first, feature_onehot((128, 96), 1))
+        handed.append(to_partner(tot.at[core], tot.at[core]))
+    for wait in handed:
+        wait()
+
+
+def finish_kernel(
+    spec_in, state_in, tot0, tot1, tot2,
+    spec_ref, state_ref, gin_ref, gbin_ref, gmid_ref, gbmid_ref, gout_ref,
+):
+    spec_ref[...] = spec_in[...]
+    state_ref[...] = state_in[...]
+    last, first = tot2[0].reshape(512, 128), tot2[1].reshape(512, 128)
+    gin_ref[...] = mm_nt(feature_onehot((96, 128), 0), first)
     gout_ref[...] = mm_nt(feature_onehot((96, 128), 0), last)
-    gmid_ref[:, :256] = tot1[...].reshape(512, 256).astype(f32)
-    gmid_ref[:, 256:] = tot2[...].reshape(512, 256).astype(f32)
+    for unit, tot in enumerate((tot0, tot1)):
+        for half in range(2):
+            at = 128 * unit + 256 * half
+            gmid_ref[:, at : at + 128] = tot[half].reshape(512, 128).astype(f32)
     pick = (iota((8, 128), 1) == USED).astype(f32).astype(bf16)
     gbin_ref[...] = mm_nt(pick, first)[:1]
     gbmid_ref[...] = mm_nt(pick, last)[:1]
@@ -460,53 +510,54 @@
     wide16 = pltpu.VMEM((512, NLON), bf16)
     wide32 = pltpu.VMEM((512, NLON), f32)
     skinny = pltpu.VMEM((128, NLON), bf16)
-    widths = (128, 256, 256, 128)
-
-    def per_piece(*leading):
-        return [pltpu.VMEM((*leading, 16, width), bf16) for width in widths]
-
+    chunk = pltpu.VMEM((N_LEV, PAD, 256), bf16)
+    unit = pltpu.VMEM((N_LAT, 16, 128), bf16)
     scratch = [
         pltpu.VMEM((576, 128), f32), pltpu.VMEM((128, NLON), f32), waves32, blocks, blocks,
         waves16, waves16, pltpu.VMEM((2 * HALF, 128), f32), waves32, waves32,
-        pltpu.VMEM((576, 128), f32), blocks, blocks,
+        pltpu.VMEM((576, 128), f32), pltpu.VMEM((128, 512), bf16), pltpu.VMEM((128, 512), bf16),
+        *[chunk] * 6,
         pltpu.VMEM((512, 128), bf16), pltpu.VMEM((128, 512), bf16), pltpu.VMEM((512, 128), bf16),
         pltpu.VMEM((512, 512), bf16), pltpu.VMEM((512, 128), f32), pltpu.VMEM((512, 128), f32),
         skinny, skinny, wide32, wide16, wide32, wide16, wide16, wide16,
         pltpu.VMEM((512, 128), f32), skinny, blocks, blocks,
-        *per_piece(N_LAT), *per_piece(N_LAT), *per_piece(), *per_piece(N_LEV), *per_piece(),
+        *[pltpu.VMEM((2, N_LAT, 16, 128), bf16)] * 3, *[unit] * 3, *[unit] * 3, *[unit] * 3,
+        *[pltpu.VMEM((16, 128), f32)] * 3, *[pltpu.VMEM((4, 16, 128), f32)] * 3,
+        *[pltpu.VMEM((16, 128), bf16)] * 3,
     ]
-    lat_sems, lev_sems = sems(N_LAT), sems(N_LEV)
-    scratch += lat_sems + lev_sems + lat_sems + lev_sems
-    scratch += lat_sems + lev_sems + lat_sems * 3
-    scratch += lev_sems * 4 + lat_sems * 4
-    spectral, state, *totals = pl.pallas_call(
+    lat_sems, lev_sems, one_sems = sems(N_LAT), sems(N_LEV), sems(1)
+    scratch += lat_sems + lev_sems + lat_sems + lev_sems * 3
+    scratch += one_sems * 2 + lev_sems + lat_sems
+    scratch += one_sems + lat_sems * 2 + lev_sems * 3 + lat_sems * 3 + one_sems * 3
+    spec_shape = like((WAVES, 2, 3, 4, TRUNC), f32)
+    state_shape = like((count, NLON), f32)
+    passed = pl.pallas_call(
         step_kernel,
-        out_shape=[
-            like((WAVES, 2, 4, 3, TRUNC), f32), like((count, NLON), f32),
-            *[like((N_LAT, 16, width), bf16) for width in widths],
-        ],
+        out_shape=[spec_shape, state_shape, *[like((2, N_LAT, 16, 128), bf16)] * 3],
         in_specs=[VMEM] * 7 + [SMEM] * 3 + [VMEM] * 5,
-        out_specs=[VMEM] * 6,
+        out_specs=[VMEM] * 5,
         scratch_shapes=scratch,
         compiler_params=pltpu.CompilerParams(collective_id=0, has_side_effects=True),
         name="step",
     )(
         prognostic.reshape(count, NLON), cotangent.reshape(count, NLON), high, low, order, lats,
         diagonal_table(), degree_table(), damping, in_scale,
-        w_in, b_in.reshape(1, 512), w_mid, b_mid.reshape(1, 512), w_out,
+        w_in.T, b_in.reshape(1, 512), w_mid, b_mid.reshape(1, 512), w_out,
     )
-    gin, gbin, gmid, gbmid, gout = pl.pallas_call(
+    spectral, state, gin, gbin, gmid, gbmid, gout = pl.pallas_call(
         finish_kernel,
         out_shape=[
-            like((512, 96), f32), like((1, 512), f32), like((512, 512), f32), like((1, 512), f32),
+            spec_shape, state_shape,
+            like((96, 512), f32), like((1, 512), f32), like((512, 512), f32), like((1, 512), f32),
             like((96, 512), f32),
         ],
-        in_specs=[VMEM] * 4,
-        out_specs=[VMEM] * 5,
+        in_specs=[VMEM] * 5,
+        out_specs=[VMEM] * 7,
         name="finish",
-    )(*totals)
+    )(*passed)
+    spectral = jnp.swapaxes(spectral, 2, 3)
     return (
-        state.reshape(prognostic.shape), spectral, gin, gbin.reshape(512), gmid, gbmid.reshape(512), gout,
+        state.reshape(prognostic.shape), spectral, gin.T, gbin.reshape(512), gmid, gbmid.reshape(512), gout,
     )
 
 

time: 84.9 us -> 72.9 us (0.86)
  Pallas kernels: 78.2 us -> 72.1 us
  local copies, waits for them, and re-layouts: 5.84 us -> 0 us
    pallas_call x2, Pallas kernels: 78.2 us -> 72.1 us  [the longest x1 69.4 us: on_device(): pl.pallas_call(step_kernel, out_shape=[spec_shape, state_shape, *[like((2...]
    unnamed x6 -> x0, local copies, waits for them, and re-layouts: 5.84 us -> none
where the time goes in v3:
time: 72.9 us; the launch traced here: 72.8 us
  Pallas kernels  72.1 us (99%)
    pallas_call x1, Pallas kernels, on_device(): pl.pallas_call(step_kernel, out_shape=[spec_shape, state_shape, *[like((2...  69.4 us
    pallas_call x1, Pallas kernels, on_device(): pl.pallas_call(finish_kernel, out_shape=[spec_shape, state_shape, like((9...  2.71 us

profile of v3, /device:TPU:1, one launch (start us, length us, event | category | flops | bytes accessed | tf_op | source)
XLA Modules:
  0.0 72.8 jit_solution(6249472604900495366)
XLA Ops:
  0.6 69.4 %step.1 = (f32[8,2,3,4,256]{4,3,2,1,0:T(4,128)}, f32[96,768]{1,0:T(8,128)}, bf16[2,32,16,128]{3,2,1,0:T(8,128)(2,1)}, bf16[2,32,16,128]{3,2,1,0:T(8,128)(2,1)}, bf16[2,32,16,128]{3,2,1,0:T(8,128)(2,1)}) custom-call(f32[96,768]{1,0:T(8,128)} %bitcast.12, bf16[96,768]{1,0:T(8,128)(2,1)} %bitcast.13, bf16[768,512]{1,0:T(8,128)(2,1)} %constant.8.clone.high_ref, ...), custom_call_target="tpu_custom_call" | custom-call | tf_op jit(solution)/shard_map/step/pallas_call | solution.py:534
  70.1 2.7 %finish.1 = (f32[8,2,3,4,256]{4,3,2,1,0:T(4,128)}, f32[96,768]{1,0:T(8,128)}, f32[96,512]{1,0:T(8,128)}, f32[1,512]{1,0:T(1,128)}, f32[512,512]{1,0:T(8,128)}, /*index=5*/f32[1,512]{1,0:T(1,128)}, f32[96,512]{1,0:T(8,128)}) custom-call(f32[8,2,3,4,256]{4,3,2,1,0:T(4,128)} %get-tuple-element.19.spec_in, f32[96,768]{1,0:T(8,128)} %get-tuple-element.20.state_in, ...), custom_call_target="tpu_custom_call" | custom-call | tf_op jit(solution)/shard_map/finish/pallas_call | solution.py:547

commit v4 on v3

--- a/solution.py
+++ b/solution.py
@@ -23,6 +23,7 @@
 SCALE_BITS = 110
 MESH = pl.DeviceIdType.MESH
 VMEM = pl.BlockSpec(memory_space=pltpu.VMEM)
+FAR = pl.BlockSpec(memory_space=pl.ANY)
 SMEM = pl.BlockSpec(memory_space=pltpu.SMEM)
 
 
@@ -97,8 +98,7 @@
             target[PAD * a : PAD * a + USED, 128 * c : 128 * (c + 1)] = picked
 
 
-def forward(x_ref, high_ref, low_ref, order_ref, lat_ref, rows, xs, fs, four_ref, lat):
-    take_rows(rows, x_ref, xs)
+def forward(high_ref, low_ref, order_ref, lat_ref, onehot_s, xs, fs, four_ref, lat):
     xh, xl = split(xs[...])
     modes = mm(xh, high_ref[...]) + mm(xl, high_ref[...]) + mm(xh, low_ref[...])
     theta = (math.pi / 256.0) * (lat_ref[...].astype(f32) + 0.5)
@@ -107,6 +107,7 @@
     picked = jnp.where(iota((ROWS * PAD, 256), 1) == row, weight, 0.0)
     modes = (modes * jnp.sum(picked, axis=1, keepdims=True)).astype(bf16)
     onehot = wave_onehot(order_ref)
+    onehot_s[...] = onehot
     for k in range(2):
         ordered = mm(modes[:, k * 256 : (k + 1) * 256], onehot)
         fs[:, 8 * k : 8 * (k + 1), :] = ordered.T.reshape(N_LAT, 8, 128)
@@ -157,7 +158,14 @@
     lax.fori_loop(0, TRUNC, step, (zero, zero, half), unroll=8)
 
 
-def analysis(four_ref, damp_ref, spec_ref, table, rs, so):
+def split_table(table, highs, lows):
+    for j in range(WAVES):
+        left = table[pl.ds(j, TRUNC, stride=WAVES), :]
+        right = table[pl.ds(HALF + j, TRUNC, stride=WAVES), :]
+        highs[j], lows[j] = split(jnp.concatenate([left, right], axis=1))
+
+
+def damp_response(damp_ref):
     pair = iota((PAD, 256), 0)
     damping = jnp.zeros((PAD, 256), f32)
     for i in range(USED):
@@ -165,8 +173,10 @@
     degree = iota((PAD, 256), 1).astype(f32)
     ratio = degree * (degree + 1.0) * (1.0 / (TRUNC * (TRUNC - 1.0)))
     response = 1.0 / (1.0 + damping * ratio * ratio)
-    response = jnp.concatenate([response, response], axis=0)
-
+    return jnp.concatenate([response, response], axis=0)
+
+
+def analysis(four_ref, response, spec_ref, highs, lows, rs, so):
     for i in range(N_LAT):
         rs[i] = four_ref[i].astype(f32)
     flat = rs.reshape(N_LAT * PAD, 128)
@@ -187,9 +197,7 @@
     made = [None] * 16
     for j in range(WAVES):
         field = jnp.concatenate([rows_of(j), rows_of(8 + j)], axis=0).astype(bf16)
-        left = table[pl.ds(j, TRUNC, stride=WAVES), :]
-        right = table[pl.ds(HALF + j, TRUNC, stride=WAVES), :]
-        high, low = split(jnp.concatenate([left, right], axis=1))
+        high, low = highs[j], lows[j]
         coeffs = (mm_nt(field, high) + mm_nt(field, low)) * response
         for k in range(2):
             for e in range(3):
@@ -215,12 +223,17 @@
             flat_out[pl.ds(4 * q + i, N_LAT, stride=PAD), :] = back[32 * i : 32 * (i + 1)]
 
 
-def mode_rows(syn_ref, order_ref, mh_s, ml_s):
-    onehot = wave_onehot(order_ref)
-    factor = jnp.where(iota((TRUNC, 128), 0) == 0, 1.0, 2.0)
+def inverse_table(high_ref, low_ref, order_ref, onehot_s, own_high, own_low):
+    factor = jnp.where(order_ref[...] == 0, 1.0, 2.0)
+    for source, target in ((high_ref, own_high), (low_ref, own_low)):
+        for k in range(2):
+            cols = slice(256 * k, 256 * (k + 1))
+            target[:, cols] = (mm(source[:, cols], onehot_s[...]) * factor).astype(bf16)
+
+
+def mode_rows(syn_ref, mh_s, ml_s):
     for k in range(2):
-        part_high, part_low = split(syn_ref[:, 8 * k : 8 * (k + 1), :].reshape(TRUNC, 128))
-        part = ((mm(onehot, part_high) + mm(onehot, part_low)) * factor).T
+        part = syn_ref[:, 8 * k : 8 * (k + 1), :].reshape(TRUNC, 128).T
         mh_s[:, 256 * k : 256 * (k + 1)], ml_s[:, 256 * k : 256 * (k + 1)] = split(part)
 
 
@@ -299,15 +312,17 @@
 
 
 def step_kernel(
-    x_ref, ct_ref, high_ref, low_ref, order_ref, lat_ref, diag_ref, deg_ref, damp_ref, scale_ref,
-    win_ref, bin_ref, wmid_ref, bmid_ref, wout_ref,
-    spec_ref, state_ref, tot0, tot1, tot2,
+    x_far, ct_far, high_far, low_far, order_ref, lat_ref, diag_ref, deg_ref, damp_ref, scale_ref,
+    win_far, bin_ref, wmid_far, bmid_ref, wout_far,
+    spec_far, state_far, tot0_far, tot1_far,
+    x_ref, ct_ref, high_ref, low_ref, win_ref, wmid_ref, wout_ref, spec_ref, state_ref, tot0, tot1,
+    onehot_s, highs, lows, own_high, own_low, local_sem,
     rows, xs, fs, up_send, up_in, four_send, four_in, table, so, syn_in, turn, mh_s, ml_s,
     in_send0, in_send1, in_send2, in_in0, in_in1, in_in2,
     win_s, wout_s, woutT_s, wmidT_s, bin_s, bmid_s, in_s, up_s, bm_s, h_in_s, slope_s, h_mid_s,
     d_mid_s, d_in_s, gbm, tend_s, tend_send, tend_in,
-    send0, send1, send2, pair0, pair1, pair2, sum0, sum1, sum2, part0, part1, part2,
-    piece0, piece1, piece2, pieces0, pieces1, pieces2, done0, done1, done2,
+    send0, send1, pair0, pair1, sum0, sum1, part0, part1,
+    piece0, piece1, pieces0, pieces1, done0, done1,
     *semaphores,
 ):
     lat, lev = lax.axis_index("lat"), lax.axis_index("lev")
@@ -330,21 +345,44 @@
         copy.start()
         return copy.wait
 
+    moves = iter(range(16))
+
+    def move(source, target):
+        copy = pltpu.make_async_copy(source, target, local_sem.at[next(moves)])
+        copy.start()
+        return copy
+
+    got_x = move(x_far, x_ref)
+    got_high = move(high_far, high_ref)
+    got_low = move(low_far, low_ref)
+    got_ct = move(ct_far, ct_ref)
+    got_weights = [move(win_far, win_ref), move(wout_far, wout_ref), move(wmid_far, wmid_ref)]
     xs[...] = jnp.zeros_like(xs)
+    got_x.wait()
+    take_rows(rows, x_ref, xs)
+    got_high.wait()
+    got_low.wait()
+    forward(high_ref, low_ref, order_ref, lat_ref, onehot_s, xs, fs, four_send, lat)
+    met()
+    wait_four = to_lat(lambda p: four_send.at[p], four_in.at[lat])
+    four_in[lat] = four_send[lat]
+    got_ct.wait()
     take_rows(rows, ct_ref, xs)
     for a in range(ROWS):
         up_send[a] = xs[PAD * a : PAD * (a + 1), :].astype(bf16)
-    forward(x_ref, high_ref, low_ref, order_ref, lat_ref, rows, xs, fs, four_send, lat)
-    met()
-    wait_four = to_lat(lambda p: four_send.at[p], four_in.at[lat])
-    wait_up = to_lev(lambda p: up_send.at[p], up_in.at[lev])
-    four_in[lat] = four_send[lat]
     up_in[lev] = up_send[lev]
     legendre_table(order_ref, lat_ref, diag_ref, deg_ref, table, lat)
+    split_table(table, highs, lows)
+    response = damp_response(damp_ref)
     wait_four()
-    analysis(four_in, damp_ref, spec_ref, table, fs, so)
+    wait_up = to_lev(lambda p: up_send.at[p], up_in.at[lev])
+    analysis(four_in, response, spec_ref, highs, lows, fs, so)
     wait_syn = to_lat(lambda p: so.at[p], syn_in.at[lat])
     syn_in[lat] = so[lat]
+    put_spec = move(spec_ref, spec_far)
+    inverse_table(high_ref, low_ref, order_ref, onehot_s, own_high, own_low)
+    for got in got_weights:
+        got.wait()
     prepare(
         win_ref, bin_ref, wmid_ref, bmid_ref, wout_ref, win_s, wout_s, woutT_s, wmidT_s, bin_s, bmid_s
     )
@@ -354,12 +392,12 @@
         scale = jnp.where(pair == i, scale_ref[i % 4, lev * 3 + i // 4], scale)
     gbm[...] = jnp.zeros_like(gbm)
     wait_syn()
-    mode_rows(syn_in, order_ref, mh_s, ml_s)
+    mode_rows(syn_in, mh_s, ml_s)
     wait_ins = []
     for c, (in_send, in_in) in enumerate(
         ((in_send0, in_in0), (in_send1, in_in1), (in_send2, in_in2))
     ):
-        inverse(mh_s, ml_s, high_ref, low_ref, scale, in_send, turn, c)
+        inverse(mh_s, ml_s, own_high, own_low, scale, in_send, turn, c)
         wait_ins.append(to_lev(lambda p, in_send=in_send: in_send.at[p], in_in.at[lev]))
         in_in[lev] = in_send[lev]
     wait_up()
@@ -395,7 +433,7 @@
     norm = 1.0 / math.sqrt(256 * NLON)
 
     def packed(value):
-        return (value * norm).astype(bf16).reshape(N_LAT, 16, 128)
+        return (value * norm).astype(bf16).reshape(N_LAT, 16, value.shape[1])
 
     def offer(send, pair):
         return to_partner(send.at[1 - core], pair)
@@ -406,16 +444,9 @@
         part[lat] = total[lat]
         return to_lat(lambda p: total.at[p], part.at[lat])
 
-    def mid_unit(send, at):
-        chosen = jnp.concatenate([h_in_s[at : at + 128, :], h_in_s[at + 256 : at + 384, :]], axis=0)
-        value = mm_nt(d_mid_s[...], chosen)
-        send[0] = packed(value[:, :128])
-        send[1] = packed(value[:, 128:])
-
-    mid_unit(send0, 0)
+    for half in range(2):
+        send0[half] = packed(mm_nt(d_mid_s[...], h_in_s[256 * half : 256 * (half + 1), :]))
     offered0 = offer(send0, pair0)
-    mid_unit(send1, 128)
-    offered1 = offer(send1, pair1)
     wait_tend = to_lev(lambda p: tend_send.at[p], tend_in.at[lev])
     tend_in[lev] = tend_send[lev]
     wait_part0 = reduce_scatter(offered0, send0, pair0, sum0, part0)
@@ -428,25 +459,21 @@
     lax.fori_loop(0, 3, delta_chunk, 0)
     bias = jnp.sum(gbm[...], axis=1, keepdims=True)
     gout = mm_nt(h_mid_s[...], up_s[...])
-    send2[0] = packed(jnp.where(iota((512, 128), 1) == USED, bias, gout))
-    send2[1] = packed(mm_nt(d_in_s[...], in_s[...]))
-    offered2 = offer(send2, pair2)
+    send1[0] = packed(jnp.where(iota((512, 128), 1) == USED, bias, gout))
+    send1[1] = packed(mm_nt(d_in_s[...], in_s[...]))
+    offered1 = offer(send1, pair1)
     wait_part1 = reduce_scatter(offered1, send1, pair1, sum1, part1)
-    wait_part2 = reduce_scatter(offered2, send2, pair2, sum2, part2)
 
     waits = []
     for wait, part, piece, pieces in (
         (wait_part0, part0, piece0, pieces0), (wait_part1, part1, piece1, pieces1),
-        (wait_part2, part2, piece2, pieces2),
     ):
         wait()
         piece[...] = total_of(part)
         waits.append(to_lev(lambda p, piece=piece: piece, pieces.at[column], stride=2))
         pieces[column] = piece[...]
     gathers = []
-    for wait, pieces, done, tot in zip(
-        waits, (pieces0, pieces1, pieces2), (done0, done1, done2), (tot0, tot1, tot2)
-    ):
+    for wait, pieces, done, tot in zip(waits, (pieces0, pieces1), (done0, done1), (tot0, tot1)):
         wait()
         done[...] = total_of(pieces).astype(bf16)
         gathers.append(to_lat(lambda p, done=done: done, tot.at[core, lat]))
@@ -463,27 +490,31 @@
             state_ref[ROWS * stored(i) : ROWS * (stored(i) + 1), 128 * c : 128 * (c + 1)] = turn[
                 at : at + ROWS, :
             ]
+    puts = [put_spec, move(state_ref, state_far)]
     handed = []
-    for wait, tot in zip(gathers, (tot0, tot1, tot2)):
+    totals = ((tot0, tot0_far), (tot1, tot1_far))
+    for wait, (tot, tot_far) in zip(gathers, totals):
         wait()
         handed.append(to_partner(tot.at[core], tot.at[core]))
-    for wait in handed:
+        puts.append(move(tot.at[core], tot_far.at[core]))
+    for wait, (tot, tot_far) in zip(handed, totals):
         wait()
+        puts.append(move(tot.at[1 - core], tot_far.at[1 - core]))
+    for put in puts:
+        put.wait()
 
 
 def finish_kernel(
-    spec_in, state_in, tot0, tot1, tot2,
+    spec_in, state_in, tot0, tot1,
     spec_ref, state_ref, gin_ref, gbin_ref, gmid_ref, gbmid_ref, gout_ref,
 ):
     spec_ref[...] = spec_in[...]
     state_ref[...] = state_in[...]
-    last, first = tot2[0].reshape(512, 128), tot2[1].reshape(512, 128)
+    last, first = tot1[0].reshape(512, 128), tot1[1].reshape(512, 128)
     gin_ref[...] = mm_nt(feature_onehot((96, 128), 0), first)
     gout_ref[...] = mm_nt(feature_onehot((96, 128), 0), last)
-    for unit, tot in enumerate((tot0, tot1)):
-        for half in range(2):
-            at = 128 * unit + 256 * half
-            gmid_ref[:, at : at + 128] = tot[half].reshape(512, 128).astype(f32)
+    for half in range(2):
+        gmid_ref[:, 256 * half : 256 * (half + 1)] = tot0[half].reshape(512, 256).astype(f32)
     pick = (iota((8, 128), 1) == USED).astype(f32).astype(bf16)
     gbin_ref[...] = mm_nt(pick, first)[:1]
     gbmid_ref[...] = mm_nt(pick, last)[:1]
@@ -511,8 +542,23 @@
     wide32 = pltpu.VMEM((512, NLON), f32)
     skinny = pltpu.VMEM((128, NLON), bf16)
     chunk = pltpu.VMEM((N_LEV, PAD, 256), bf16)
-    unit = pltpu.VMEM((N_LAT, 16, 128), bf16)
+    widths = (256, 128)
+
+    def per_unit(dtype, *leading):
+        return [pltpu.VMEM((*leading, 16, width), dtype) for width in widths]
+
+    spec_shape = like((WAVES, 2, 3, 4, TRUNC), f32)
+    state_shape = like((count, NLON), f32)
+    total_shapes = [like((2, N_LAT, 16, width), bf16) for width in widths]
     scratch = [
+        pltpu.VMEM((count, NLON), f32), pltpu.VMEM((count, NLON), bf16),
+        pltpu.VMEM((NLON, 512), bf16), pltpu.VMEM((NLON, 512), bf16),
+        pltpu.VMEM((96, 512), bf16), pltpu.VMEM((512, 512), bf16), pltpu.VMEM((96, 512), bf16),
+        pltpu.VMEM(spec_shape.shape, f32), pltpu.VMEM(state_shape.shape, f32),
+        *per_unit(bf16, 2, N_LAT),
+        pltpu.VMEM((TRUNC, TRUNC), bf16),
+        pltpu.VMEM((WAVES, TRUNC, 256), bf16), pltpu.VMEM((WAVES, TRUNC, 256), bf16),
+        pltpu.VMEM((NLON, 512), bf16), pltpu.VMEM((NLON, 512), bf16), pltpu.SemaphoreType.DMA((16,)),
         pltpu.VMEM((576, 128), f32), pltpu.VMEM((128, NLON), f32), waves32, blocks, blocks,
         waves16, waves16, pltpu.VMEM((2 * HALF, 128), f32), waves32, waves32,
         pltpu.VMEM((576, 128), f32), pltpu.VMEM((128, 512), bf16), pltpu.VMEM((128, 512), bf16),
@@ -521,21 +567,18 @@
         pltpu.VMEM((512, 512), bf16), pltpu.VMEM((512, 128), f32), pltpu.VMEM((512, 128), f32),
         skinny, skinny, wide32, wide16, wide32, wide16, wide16, wide16,
         pltpu.VMEM((512, 128), f32), skinny, blocks, blocks,
-        *[pltpu.VMEM((2, N_LAT, 16, 128), bf16)] * 3, *[unit] * 3, *[unit] * 3, *[unit] * 3,
-        *[pltpu.VMEM((16, 128), f32)] * 3, *[pltpu.VMEM((4, 16, 128), f32)] * 3,
-        *[pltpu.VMEM((16, 128), bf16)] * 3,
+        *per_unit(bf16, 2, N_LAT), *per_unit(bf16, N_LAT) * 3,
+        *per_unit(f32), *per_unit(f32, 4), *per_unit(bf16),
     ]
     lat_sems, lev_sems, one_sems = sems(N_LAT), sems(N_LEV), sems(1)
     scratch += lat_sems + lev_sems + lat_sems + lev_sems * 3
-    scratch += one_sems * 2 + lev_sems + lat_sems
-    scratch += one_sems + lat_sems * 2 + lev_sems * 3 + lat_sems * 3 + one_sems * 3
-    spec_shape = like((WAVES, 2, 3, 4, TRUNC), f32)
-    state_shape = like((count, NLON), f32)
+    scratch += one_sems + lev_sems + lat_sems
+    scratch += one_sems + lat_sems + lev_sems * 2 + lat_sems * 2 + one_sems * 2
     passed = pl.pallas_call(
         step_kernel,
-        out_shape=[spec_shape, state_shape, *[like((2, N_LAT, 16, 128), bf16)] * 3],
-        in_specs=[VMEM] * 7 + [SMEM] * 3 + [VMEM] * 5,
-        out_specs=[VMEM] * 5,
+        out_shape=[spec_shape, state_shape, *total_shapes],
+        in_specs=[FAR] * 4 + [VMEM] * 3 + [SMEM] * 3 + [FAR, VMEM, FAR, VMEM, FAR],
+        out_specs=[FAR] * 4,
         scratch_shapes=scratch,
         compiler_params=pltpu.CompilerParams(collective_id=0, has_side_effects=True),
         name="step",
@@ -551,7 +594,7 @@
             like((96, 512), f32), like((1, 512), f32), like((512, 512), f32), like((1, 512), f32),
             like((96, 512), f32),
         ],
-        in_specs=[VMEM] * 5,
+        in_specs=[VMEM] * 4,
         out_specs=[VMEM] * 7,
         name="finish",
     )(*passed)

time: 72.9 us -> 70.2 us (0.963)
  Pallas kernels: 72.1 us -> 69.4 us
    pallas_call x1, Pallas kernels: 69.4 us -> 66.7 us  [on_device(): pl.pallas_call(step_kernel, out_shape=[spec_shape, state_shape, *total_sh...]
where the time goes in v4:
time: 70.2 us; the launch traced here: 70.1 us
  Pallas kernels  69.4 us (99%)
    pallas_call x1, Pallas kernels, on_device(): pl.pallas_call(step_kernel, out_shape=[spec_shape, state_shape, *total_sh...  66.7 us
    pallas_call x1, Pallas kernels, on_device(): pl.pallas_call(finish_kernel, out_shape=[spec_shape, state_shape, like((9...  2.75 us

profile of v4, /device:TPU:1, one launch (start us, length us, event | category | flops | bytes accessed | tf_op | source)
XLA Modules:
  0.0 70.1 jit_solution(5386696312223343707)
XLA Ops:
  0.6 66.7 %step.1 = (f32[8,2,3,4,256]{4,3,2,1,0:T(4,128)}, f32[96,768]{1,0:T(8,128)}, bf16[2,32,16,256]{3,2,1,0:T(8,128)(2,1)}, bf16[2,32,16,128]{3,2,1,0:T(8,128)(2,1)}) custom-call(f32[96,768]{1,0:T(8,128)} %bitcast.12, bf16[96,768]{1,0:T(8,128)(2,1)} %bitcast.13, bf16[768,512]{1,0:T(8,128)(2,1)} %constant.8.clone.high_far, bf16[768,512]{1,0:T(8,128)(2,1)} %constant.9.clone.low_far, ...), custom_call_target="tpu_custom_call" | custom-call | tf_op jit(solution)/shard_map/step/pallas_call | solution.py:577
  67.3 2.7 %finish.1 = (f32[8,2,3,4,256]{4,3,2,1,0:T(4,128)}, f32[96,768]{1,0:T(8,128)}, f32[96,512]{1,0:T(8,128)}, f32[1,512]{1,0:T(1,128)}, f32[512,512]{1,0:T(8,128)}, /*index=5*/f32[1,512]{1,0:T(1,128)}, f32[96,512]{1,0:T(8,128)}) custom-call(f32[8,2,3,4,256]{4,3,2,1,0:T(4,128)} %get-tuple-element.18.spec_in, f32[96,768]{1,0:T(8,128)} %get-tuple-element.19.state_in, ...), custom_call_target="tpu_custom_call" | custom-call | tf_op jit(solution)/shard_map/finish/pallas_call | solution.py:590

commit v5 on v4

--- a/solution.py
+++ b/solution.py
@@ -444,11 +444,11 @@
         part[lat] = total[lat]
         return to_lat(lambda p: total.at[p], part.at[lat])
 
+    wait_tend = to_lev(lambda p: tend_send.at[p], tend_in.at[lev])
+    tend_in[lev] = tend_send[lev]
     for half in range(2):
         send0[half] = packed(mm_nt(d_mid_s[...], h_in_s[256 * half : 256 * (half + 1), :]))
     offered0 = offer(send0, pair0)
-    wait_tend = to_lev(lambda p: tend_send.at[p], tend_in.at[lev])
-    tend_in[lev] = tend_send[lev]
     wait_part0 = reduce_scatter(offered0, send0, pair0, sum0, part0)
 
     def delta_chunk(c, _):
@@ -572,7 +572,7 @@
     ]
     lat_sems, lev_sems, one_sems = sems(N_LAT), sems(N_LEV), sems(1)
     scratch += lat_sems + lev_sems + lat_sems + lev_sems * 3
-    scratch += one_sems + lev_sems + lat_sems
+    scratch += lev_sems + one_sems + lat_sems
     scratch += one_sems + lat_sems + lev_sems * 2 + lat_sems * 2 + one_sems * 2
     passed = pl.pallas_call(
         step_kernel,

time: 70.2 us -> 69.8 us (level)
  no operation moved by 1% of the time
where the time goes in v5:
time: 69.8 us; the launch traced here: 69.6 us
  Pallas kernels  69 us (99%)
    pallas_call x1, Pallas kernels, on_device(): pl.pallas_call(step_kernel, out_shape=[spec_shape, state_shape, *total_sh...  66.2 us
    pallas_call x1, Pallas kernels, on_device(): pl.pallas_call(finish_kernel, out_shape=[spec_shape, state_shape, like((9...  2.75 us

profile of v5, /device:TPU:1, one launch (start us, length us, event | category | flops | bytes accessed | tf_op | source)
XLA Modules:
  0.0 69.6 jit_solution(10904617339983825076)
XLA Ops:
  0.6 66.2 %step.1 = (f32[8,2,3,4,256]{4,3,2,1,0:T(4,128)}, f32[96,768]{1,0:T(8,128)}, bf16[2,32,16,256]{3,2,1,0:T(8,128)(2,1)}, bf16[2,32,16,128]{3,2,1,0:T(8,128)(2,1)}) custom-call(f32[96,768]{1,0:T(8,128)} %bitcast.12, bf16[96,768]{1,0:T(8,128)(2,1)} %bitcast.13, bf16[768,512]{1,0:T(8,128)(2,1)} %constant.8.clone.high_far, bf16[768,512]{1,0:T(8,128)(2,1)} %constant.9.clone.low_far, ...), custom_call_target="tpu_custom_call" | custom-call | tf_op jit(solution)/shard_map/step/pallas_call | solution.py:577
  66.9 2.7 %finish.1 = (f32[8,2,3,4,256]{4,3,2,1,0:T(4,128)}, f32[96,768]{1,0:T(8,128)}, f32[96,512]{1,0:T(8,128)}, f32[1,512]{1,0:T(1,128)}, f32[512,512]{1,0:T(8,128)}, /*index=5*/f32[1,512]{1,0:T(1,128)}, f32[96,512]{1,0:T(8,128)}) custom-call(f32[8,2,3,4,256]{4,3,2,1,0:T(4,128)} %get-tuple-element.18.spec_in, f32[96,768]{1,0:T(8,128)} %get-tuple-element.19.state_in, ...), custom_call_target="tpu_custom_call" | custom-call | tf_op jit(solution)/shard_map/finish/pallas_call | solution.py:590
